TPU v7x, 256 devices: a whole 4x4x8 slice. The times are simulated.
256 devices in a mesh: ctx: 16 (over y, x), tp: 16 (over z, core).
Axes of the slice: x: 4, y: 4, z: 8, core: 2. Of those that a mesh axis runs over, the one named last changes fastest.
Arguments:
- residual: bfloat16 [2048, 6144], P('ctx', 'tp'), may hold values from -65 to 65
- query_rows: bfloat16 [2048, 8192], P('ctx', 'tp'), may hold values from -6 to 6
- key_rows: bfloat16 [2048, 8192], P('ctx', 'tp'), may hold values from -6 to 6
- value_rows: bfloat16 [2048, 8192], P('ctx', 'tp'), may hold values from -6 to 6
- head_rates: float32 [64], replicated, may hold values from 0 to 1
- doc_lengths: int32 [4], replicated, may hold values from 1 to 1024, 2048 in all
- attn_gain: float32 [8192], P('tp'), may hold values from 0.1 to 1.9
- out_weight: bfloat16 [8192, 6144], P('tp', 'ctx'), may hold values from -0.09375 to 0.09375
- moe_gain: float32 [6144], P('tp'), may hold values from 0.1 to 1.9
- expert_ids: int32 [2048, 2], P('ctx'), may hold values from 0 to 15, all different within a row; in each aligned block of 128 rows (0 to 127, 128 to 255, ...) at most 24 rows name the same one
- expert_weights: float32 [2048, 2], P('ctx'), may hold values from 0.2 to 1
- gate_weight: bfloat16 [16, 6144, 4608], P('ctx', None, 'tp'), may hold values from -0.078125 to 0.078125
- up_weight: bfloat16 [16, 6144, 4608], P('ctx', None, 'tp'), may hold values from -0.078125 to 0.078125
- down_weight: bfloat16 [16, 4608, 6144], P('ctx', 'tp'), may hold values from -0.125 to 0.125
Outputs:
- output: bfloat16 [2048, 6144], P('ctx', 'tp')
Inputs may be any that keep to these rules, and one draw needn't show every extreme that they name: `expert_ids`: each token names 2 different experts; among the tokens of one device (aligned blocks of 128 rows) no expert is named more than 24 times, a bound that some block reaches. `doc_lengths`: the longest document holds exactly 1024 positions.
All inputs are finite; a program needn't handle non-finite values.
Results may differ from a plain program's by a relative error of at most 0.015.
Values may be sent and summed in bfloat16 or wider, within the bound.
A program may use at most 64 MiB of HBM per device.

v0:
```python
import jax
import jax.numpy as jnp
from jax import lax
from jax.sharding import Mesh
from jax.sharding import PartitionSpec as P

D = 6144
HD = 128
TOP = 2
CTX = ("ctx_0", "ctx_1")
TP = ("tp_0", "tp_1")


def nothing_yet(x, identity):
    return jax.tree.map(
        lambda part, zero: jnp.zeros_like(part) + jnp.asarray(zero, part.dtype), x, identity
    )


def carried_in(x, axes, combine, identity):
    before = start = nothing_yet(x, identity)
    running = x
    for axis in reversed(axes):
        peers, index = (lax.axis_size(axis), lax.axis_index(axis))
        pieces = jax.tree.map(
            lambda part, kind: lax.all_gather(part.astype(kind), axis),
            running,
            (jnp.bfloat16, jnp.bfloat16),
        )
        inside, running = (start, start)
        for k in range(peers):
            passed = k < index
            running = combine(
                running, jax.tree.map(lambda part, own: part[k].astype(own.dtype), pieces, x)
            )
            inside = jax.tree.map(lambda new, old: jnp.where(passed, new, old), running, inside)
        before = combine(inside, before)
    return before


def cut_along(x, dim, peers):
    lengths = x.shape
    tiles = x.reshape(*lengths[:dim], peers, lengths[dim] // peers, *lengths[dim + 1 :])
    return jnp.moveaxis(tiles, dim, 0)


def sum_at_owner(x, axis, dim):
    peers = lax.axis_size(axis)
    tiles = lax.all_to_all(cut_along(x, dim, peers), axis, 0, 0, tiled=True)
    return jnp.sum(tiles.astype(jnp.float32), axis=0)


def sent_to_all(x, axis):
    peers = lax.axis_size(axis)
    return lax.all_to_all(jnp.broadcast_to(x[None], (peers, *x.shape)), axis, 0, 0, tiled=True)


def taken_together(x, axis):
    return sent_to_all(x, axis).sum(axis=0)


def summed_rows(x, chips, core, dim):
    sizes = (lax.axis_size(chips), lax.axis_size(core))
    tiles = cut_along(x, dim, sizes[0] * sizes[1])
    inside = tiles.shape[1:]
    tiles = tiles.reshape(*sizes, *inside).swapaxes(0, 1).reshape(-1, *inside)
    tiles = lax.psum_scatter(tiles, core, scatter_dimension=0, tiled=True)
    return lax.psum_scatter(tiles, chips, scatter_dimension=0, tiled=True)[0]


def segment_of(doc_lengths, positions):
    doc_ends = jnp.cumsum(doc_lengths)
    doc_starts = doc_ends - doc_lengths
    return jnp.sum((positions[:, None] >= doc_starts[None, :]).astype(jnp.int32), axis=1) - 1


def local_attention(query_h, key_h, value_h, head_decay, segments, seg_before):
    length = query_h.shape[0]
    offsets = jnp.arange(length, dtype=jnp.int32)
    distance = (offsets[:, None] - offsets[None, :]).astype(jnp.float32)
    allowed = (offsets[:, None] >= offsets[None, :]) & (segments[:, None] == segments[None, :])
    decay_mask = jnp.where(
        allowed[None], jnp.exp(-head_decay[:, None, None] * jnp.maximum(distance, 0.0)[None]), 0.0
    )
    scores = jnp.einsum("ihd,jhd->hij", query_h, key_h, preferred_element_type=jnp.float32)
    weights = (scores * decay_mask).astype(jnp.bfloat16)
    within = jnp.einsum("hij,jhd->ihd", weights, value_h, preferred_element_type=jnp.float32)
    last_seg = segments[length - 1]
    fading = jnp.where(
        (segments == last_seg)[:, None],
        jnp.exp(-head_decay[None, :] * (length - 1 - offsets).astype(jnp.float32)[:, None]),
        0.0,
    )
    weighted_keys = key_h.astype(jnp.float32) * fading[:, :, None]
    local_state = jnp.einsum(
        "jhd,jhe->hde", weighted_keys, value_h.astype(jnp.float32), precision=lax.Precision.HIGHEST
    )
    carry_factor = jnp.where(last_seg == seg_before, jnp.exp(-head_decay * length), 0.0)
    reaching = jnp.where(
        (segments == seg_before)[:, None],
        jnp.exp(-head_decay[None, :] * (offsets + 1).astype(jnp.float32)[:, None]),
        0.0,
    )
    return (within, local_state, carry_factor, reaching)


def shards(
    residual,
    query_rows,
    key_rows,
    value_rows,
    head_rates,
    doc_lengths,
    attn_gain,
    out_weight,
    moe_gain,
    expert_ids,
    expert_weights,
    gate_weight,
    up_weight,
    down_weight,
):
    length = query_rows.shape[0]
    local_heads = attn_gain.shape[0] // HD
    ctx_index = lax.axis_index(CTX)
    tp_index = lax.axis_index(TP)
    head_decay = lax.dynamic_slice_in_dim(head_rates, tp_index * local_heads, local_heads)
    first_pos = ctx_index * length
    positions = first_pos + jnp.arange(length, dtype=jnp.int32)
    segments = segment_of(doc_lengths, positions)
    seg_before = segment_of(doc_lengths, jnp.reshape(first_pos - 1, (1,)))[0]
    query_h = query_rows.reshape(length, local_heads, HD)
    key_h = key_rows.reshape(length, local_heads, HD)
    value_h = value_rows.reshape(length, local_heads, HD)
    within, local_state, carry_factor, reaching = local_attention(
        query_h, key_h, value_h, head_decay, segments, seg_before
    )

    def combine(earlier, later_one):
        return (earlier[0] * later_one[0], later_one[0][:, None, None] * earlier[1] + later_one[1])

    prefix = carried_in(
        (carry_factor, local_state),
        CTX,
        combine,
        (jnp.ones_like(carry_factor), jnp.zeros_like(local_state)),
    )
    incoming = prefix[1]
    inter = (
        jnp.einsum(
            "ihd,hde->ihe", query_h.astype(jnp.float32), incoming, precision=lax.Precision.HIGHEST
        )
        * reaching[:, :, None]
    )
    mixed_out = within + inter
    scaled = mixed_out * lax.rsqrt(jnp.mean(mixed_out * mixed_out, axis=-1, keepdims=True) + 1e-06)
    heads_out = (scaled.reshape(length, local_heads * HD) * attn_gain).astype(jnp.bfloat16)
    partial_out = jnp.dot(
        heads_out,
        lax.all_gather(out_weight, CTX, axis=1, tiled=True),
        preferred_element_type=jnp.float32,
    )
    attn_out = sum_at_owner(partial_out.astype(jnp.bfloat16), TP, 1)
    hidden_state = (residual.astype(jnp.float32) + attn_out).astype(jnp.bfloat16)
    widened = hidden_state.astype(jnp.float32)
    sum_squares = taken_together(jnp.sum(widened * widened, axis=1), TP)
    moe_input = (widened * lax.rsqrt(sum_squares / D + 1e-05)[:, None] * moe_gain).astype(
        jnp.bfloat16
    )
    experts = lax.axis_size(CTX)
    capacity = 3 * length * TOP // (2 * experts)
    flat_ids = expert_ids.reshape(-1)
    onehot = (flat_ids[:, None] == jnp.arange(experts, dtype=jnp.int32)[None, :]).astype(jnp.int32)
    slot_ranks = jnp.sum((jnp.cumsum(onehot, axis=0) - onehot) * onehot, axis=1)
    slot_index = flat_ids * capacity + slot_ranks
    source_row = (
        jnp.zeros((experts * capacity,), jnp.int32)
        .at[slot_index]
        .set(jnp.arange(length * TOP, dtype=jnp.int32) // TOP)
    )
    occupied = jnp.zeros((experts * capacity,), jnp.bool_).at[slot_index].set(True)
    picked_rows = jnp.where(
        occupied[:, None], moe_input[source_row], jnp.zeros((), moe_input.dtype)
    )
    arrived = lax.all_gather(
        lax.all_to_all(
            picked_rows.reshape(experts, capacity, moe_input.shape[1]),
            CTX,
            split_axis=0,
            concat_axis=0,
            tiled=True,
        ),
        TP,
        axis=2,
        tiled=True,
    )
    flat_in = arrived.reshape(-1, arrived.shape[2])
    gate_pre = jnp.dot(flat_in, gate_weight[0], preferred_element_type=jnp.float32)
    up_pre = jnp.dot(flat_in, up_weight[0], preferred_element_type=jnp.float32)
    activated = (jax.nn.silu(gate_pre) * up_pre).astype(jnp.bfloat16)
    down_term = jnp.dot(activated, down_weight[0], preferred_element_type=jnp.float32)
    reduced = summed_rows(down_term.astype(jnp.bfloat16), "tp_0", "tp_1", 1).astype(jnp.float32)
    outbound = reduced.astype(jnp.bfloat16).reshape(
        arrived.shape[0], arrived.shape[1], reduced.shape[1]
    )
    returned = lax.all_to_all(outbound, CTX, split_axis=0, concat_axis=0, tiled=True)
    returned_flat = returned.reshape(experts * capacity, returned.shape[2])
    gathered_out = (
        returned_flat[slot_index].reshape(length, TOP, returned.shape[2]).astype(jnp.float32)
    )
    mixture = jnp.sum(gathered_out * expert_weights[:, :, None], axis=1)
    return (widened + mixture).astype(jnp.bfloat16)


def solution(mesh):
    finer = Mesh(mesh.devices.reshape(4, 4, 8, 2), ("ctx_0", "ctx_1", "tp_0", "tp_1"))
    placed = (
        P(CTX, TP),
        P(CTX, TP),
        P(CTX, TP),
        P(CTX, TP),
        P(),
        P(),
        P(TP),
        P(TP, CTX),
        P(TP),
        P(CTX, None),
        P(CTX, None),
        P(CTX, None, TP),
        P(CTX, None, TP),
        P(CTX, TP, None),
    )
    return jax.shard_map(shards, mesh=finer, in_specs=placed, out_specs=P(CTX, TP), check_vma=False)
```

profile of v0, /device:TPU:1, one launch (start us, length us, event | category | flops | bytes accessed | tf_op | source)
XLA Modules:
  0.0 316.1 jit_solution(3398791720834157552)
XLA Ops:
  15.1 9.3 %all-reduce = bf16[16]{0:T(256)(128)(2,1)S(1)} all-reduce(bf16[16]{0:T(256)(128)(2,1)S(1)} %dynamic-update-slice), channel_id=2, replica_groups=mesh['ctx_0'=4,'ctx_1'=4,'tp_0'=8,'tp_1'=2] {'ctx_1'}, use_global_device_ids=true, to_apply=%add | all-reduce | flops 16 | bytes 64
  25.0 8.3 %all-gather.2 = bf16[4,1,4]{2,1,0:T(2,128)(2,1)S(1)} all-gather(bf16[1,1,4]{2,1,0:T(2,128)(2,1)S(1)} %bitcast.205), channel_id=1, replica_groups=mesh['ctx_0'=4,'ctx_1'=4,'tp_0'=8,'tp_1'=2] {'ctx_0'}, dimensions={0}, use_global_device_ids=true | all-gather | bytes 40 | tf_op jit(solution)/shard_map/all_gather | solution.py:26
  38.9 10.6 %all-gather.1 = bf16[16,128,128]{2,1,0:T(8,128)(2,1)S(1)} all-gather(bf16[4,128,128]{2,1,0:T(8,128)(2,1)S(1)} %convolution_convert_fusion.2), channel_id=3, replica_groups=mesh['ctx_0'=4,'ctx_1'=4,'tp_0'=8,'tp_1'=2] {'ctx_1'}, dimensions={0}, use_global_device_ids=true | all-gather | bytes 655360 | tf_op jit(solution)/shard_map/all_gather | solution.py:26
  50.4 13.6 %all_gather.31 = bf16[4,4,128,128]{3,2,1,0:T(8,128)(2,1)} all-gather(bf16[1,4,128,128]{3,2,1,0:T(8,128)(2,1)S(1)} %fusion.28), channel_id=1, replica_groups=mesh['ctx_0'=4,'ctx_1'=4,'tp_0'=8,'tp_1'=2] {'ctx_0'}, dimensions={0}, use_global_device_ids=true | all-gather | bytes 655360 | tf_op jit(solution)/shard_map/all_gather | solution.py:26
  66.0 2.1 convolution_bitcast_fusion.1
  68.1 2.2 multiply_reduce_fusion.1
  71.2 16.8 %all-gather.6.cloned.1.call-done = bf16[512,6144]{1,0:T(8,128)(2,1)} async-done(((bf16[512,384]{1,0:T(8,128)(2,1)}), bf16[512,6144]{1,0:T(8,128)(2,1)}) %all-gather.6.cloned.1.call-update) | async-done | bytes 6291472 | tf_op jit(solution)/shard_map/all_gather | solution.py:160
  88.0 3.9 %convolution_convert_fusion.1 = bf16[128,6144]{1,0:T(8,128)(2,1)S(1)} fusion(bf16[128,512]{0,1:T(8,128)(2,1)} %fusion.37, bf16[512,6144]{1,0:T(8,128)(2,1)} %all-gather.6.cloned.1.call-done), kind=kOutput, calls=%fused_computation.5 | convolution fusion | flops 806092800 | bytes 7995392 | tf_op jit(solution)/shard_map/dot_general | solution.py:158
  93.3 8.3 %all-to-all-start = ((bf16[16,128,384]{2,1,0:T(8,128)(2,1)}), bf16[16,128,384]{2,1,0:T(8,128)(2,1)}, u32[]{:S(2)}, u32[]{:S(2)}) async-start(bf16[16,128,384]{2,1,0:T(8,128)(2,1)} %bitcast.194), calls=%async_computation | async-start | bytes 3145728 | tf_op jit(solution)/shard_map/all_to_all | solution.py:49
  117.8 22.5 %all-to-all-done = bf16[16,128,384]{2,1,0:T(8,128)(2,1)} async-done(((bf16[16,128,384]{2,1,0:T(8,128)(2,1)}), bf16[16,128,384]{2,1,0:T(8,128)(2,1)}, u32[]{:S(2)}, u32[]{:S(2)}) %all-to-all-start) | async-done | bytes 1572896 | tf_op jit(solution)/shard_map/all_to_all | solution.py:49
  144.0 4.1 %all-to-all-start.1 = ((f32[16,1,128]{2,1,0:T(1,128)}), f32[16,1,128]{2,1,0:T(1,128)S(1)}, u32[]{:S(2)}, u32[]{:S(2)}) async-start(f32[16,1,128]{2,1,0:T(1,128)} %broadcast_in_dim.65), calls=%async_computation.1 | async-start | bytes 16384 | tf_op jit(solution)/shard_map/all_to_all | solution.py:55
  148.2 2.1 scatter_custom_fusion
  151.0 4.2 %all-to-all-done.1 = f32[16,1,128]{2,1,0:T(1,128)S(1)} async-done(((f32[16,1,128]{2,1,0:T(1,128)}), f32[16,1,128]{2,1,0:T(1,128)S(1)}, u32[]{:S(2)}, u32[]{:S(2)}) %all-to-all-start.1) | async-done | bytes 8224 | tf_op jit(solution)/shard_map/all_to_all | solution.py:55
  158.2 3.3 %gather_fusion = bf16[384,384]{1,0:T(8,128)(2,1)} fusion(bf16[128,384]{1,0:T(8,128)(2,1)} %fusion.49, s32[1024]{0:T(1024)S(1)} %pad_clamp_fusion.1), kind=kCustom, calls=%fused_computation | custom fusion | bytes 591360 | tf_op jit(solution)/shard_map/gather | solution.py:183
  162.5 13.7 %all_to_all.21 = bf16[16,24,384]{2,1,0:T(8,128)(2,1)} all-to-all(bf16[16,24,384]{2,1,0:T(8,128)(2,1)S(1)} %broadcast_select_fusion), channel_id=1, replica_groups=mesh['ctx_0'=4,'ctx_1'=4,'tp_0'=8,'tp_1'=2] {'ctx_0','ctx_1'}, dimensions={0} | all-to-all | bytes 589824 | tf_op jit(solution)/shard_map/all_to_all | solution.py:186
  176.5 37.7 %all-gather.8.cloned.1.call-done = bf16[16,24,6144]{2,1,0:T(8,128)(2,1)} async-done(((bf16[16,24,384]{2,1,0:T(8,128)(2,1)}), bf16[16,24,6144]{2,1,0:T(8,128)(2,1)}) %all-gather.8.cloned.1.call-update) | async-done | bytes 4718608 | tf_op jit(solution)/shard_map/all_gather | solution.py:185
  214.2 5.6 %fusion.3 = f32[384,288]{0,1:T(8,128)S(1)} fusion(bf16[384,6144]{1,0:T(8,128)(2,1)} %bitcast.207, bf16[1,6144,288]{1,2,0:T(8,128)(2,1)} %param.25), kind=kOutput, calls=%fused_computation.10 | convolution fusion | flops 1358954496 | bytes 8699904 | tf_op jit(solution)/shard_map/dot_general | solution.py:198
  222.1 2.9 convolution_convert_fusion
  225.7 2.7 copy.89
  228.4 17.0 %reduce-scatter.3.cloned.1.call-done = bf16[8,384,384]{2,1,0:T(8,128)(2,1)} async-done(((bf16[16,384,384]{2,1,0:T(8,128)(2,1)}), bf16[8,384,384]{2,1,0:T(8,128)(2,1)}) %reduce-scatter.3.cloned.1.call-update) | async-done | bytes 2359312 | tf_op jit(solution)/shard_map/reduce_scatter | solution.py:67
  245.4 42.0 %reduce-scatter.5.cloned.1.call-done = bf16[1,384,384]{2,1,0:T(8,128)(2,1)} async-done(((bf16[8,384,384]{2,1,0:T(8,128)(2,1)}), bf16[1,384,384]{2,1,0:T(8,128)(2,1)}) %reduce-scatter.5.cloned.1.call-update) | async-done | bytes 294928 | tf_op jit(solution)/shard_map/reduce_scatter | solution.py:68
  287.4 6.6 %all-to-all-start.3 = ((bf16[16,24,384]{2,1,0:T(8,128)(2,1)}), bf16[16,24,384]{2,1,0:T(8,128)(2,1)}, u32[]{:S(2)}, u32[]{:S(2)}) async-start(bf16[16,24,384]{2,1,0:T(8,128)(2,1)} %bitcast.199), calls=%async_computation.5 | async-start | bytes 589824 | tf_op jit(solution)/shard_map/all_to_all | solution.py:206
  294.8 7.0 %all-to-all-done.3 = bf16[16,24,384]{2,1,0:T(8,128)(2,1)} async-done(((bf16[16,24,384]{2,1,0:T(8,128)(2,1)}), bf16[16,24,384]{2,1,0:T(8,128)(2,1)}, u32[]{:S(2)}, u32[]{:S(2)}) %all-to-all-start.3) | async-done | bytes 294944 | tf_op jit(solution)/shard_map/all_to_all | solution.py:206
  301.8 2.8 gather_fusion.1
  (99 shorter events, 51.6 us)
Async XLA Ops:
  6.5 215.5 %copy-start = (bf16[1,288,6144]{2,1,0:T(8,128)(2,1)S(1)}, bf16[1,288,6144]{2,1,0:T(8,128)(2,1)}, u32[]{:S(2)}) copy-start(bf16[1,288,6144]{2,1,0:T(8,128)(2,1)} %param.27) | copy-start | bytes 10616836
  6.5 81.5 %all-gather.6.cloned.1.call-start = ((), (), s32[]{:S(2)}) async-start(), calls=%async_computation.6 | async-start | bytes 6684672 | tf_op jit(solution)/shard_map/all_gather | solution.py:160
  9.8 1.2 copy-start.13
  9.8 0.6 copy-start.10
  14.9 49.7 %copy-start.11 = (f32[4]{0:T(128)}, f32[4]{0:T(128)S(1)}, u32[]{:S(2)}) copy-start(f32[4]{0:T(128)S(1)} %get-tuple-element.10) | copy-start | bytes 52
  25.0 39.6 %copy-start.9 = (f32[4]{0:T(128)}, f32[4]{0:T(128)S(1)}, u32[]{:S(2)}) copy-start(f32[4]{0:T(128)S(1)} %get-tuple-element.16) | copy-start | bytes 52
  49.4 0.8 copy-start.1
  49.5 15.7 %copy-start.6 = (f32[4]{0:T(128)}, f32[4]{0:T(128)S(1)}, u32[]{:S(2)}) copy-start(f32[4]{0:T(128)S(1)} %get-tuple-element.21) | copy-start | bytes 52
  49.5 15.7 %copy-start.7 = (f32[4]{0:T(128)}, f32[4]{0:T(128)S(1)}, u32[]{:S(2)}) copy-start(f32[4]{0:T(128)S(1)} %get-tuple-element.22) | copy-start | bytes 52
  49.5 15.7 %copy-start.8 = (f32[4]{0:T(128)}, f32[4]{0:T(128)S(1)}, u32[]{:S(2)}) copy-start(f32[4]{0:T(128)S(1)} %get-tuple-element.23) | copy-start | bytes 52
  68.1 2.3 copy-start.5
  91.9 9.7 %copy-start.2 = (s32[128,2]{0,1:T(2,128)S(1)}, s32[128,2]{0,1:T(2,128)}, u32[]{:S(2)}) copy-start(s32[128,2]{0,1:T(2,128)} %param.23) | copy-start | bytes 3076
  93.3 46.9 %all-to-all-start = ((bf16[16,128,384]{2,1,0:T(8,128)(2,1)}), bf16[16,128,384]{2,1,0:T(8,128)(2,1)}, u32[]{:S(2)}, u32[]{:S(2)}) async-start(bf16[16,128,384]{2,1,0:T(8,128)(2,1)} %bitcast.194), calls=%async_computation | async-start | bytes 3145728 | tf_op jit(solution)/shard_map/all_to_all | solution.py:49
  116.2 27.9 %copy-start.3 = (s32[256,1]{0,1:T(1,128)}, s32[256,1]{0,1:T(1,128)S(1)}, u32[]{:S(2)}) copy-start(s32[256,1]{0,1:T(1,128)S(1)} %compare_select_fusion) | copy-start | bytes 3076
  144.0 11.2 %all-to-all-start.1 = ((f32[16,1,128]{2,1,0:T(1,128)}), f32[16,1,128]{2,1,0:T(1,128)S(1)}, u32[]{:S(2)}, u32[]{:S(2)}) async-start(f32[16,1,128]{2,1,0:T(1,128)} %broadcast_in_dim.65), calls=%async_computation.1 | async-start | bytes 16384 | tf_op jit(solution)/shard_map/all_to_all | solution.py:55
  148.2 66.0 %all-gather.8.cloned.1.call-start = ((), (), s32[]{:S(2)}) async-start(), calls=%async_computation.7 | async-start | bytes 5013504 | tf_op jit(solution)/shard_map/all_gather | solution.py:185
  176.2 69.2 %reduce-scatter.3.cloned.1.call-start = ((), (), s32[]{:S(2)}) async-start(), calls=%async_computation.8 | async-start | bytes 7077888 | tf_op jit(solution)/shard_map/reduce_scatter | solution.py:67
  214.2 5.6 %copy-start.14 = (bf16[16,24,6144]{2,1,0:T(8,128)(2,1)S(1)}, bf16[16,24,6144]{2,1,0:T(8,128)(2,1)}, u32[]{:S(2)}) copy-start(bf16[16,24,6144]{2,1,0:T(8,128)(2,1)} %all-gather.8.cloned.1.call-done) | copy-start | bytes 14155780
  214.2 5.9 %copy-start.15 = (bf16[1,6144,288]{1,2,0:T(8,128)(2,1)S(1)}, bf16[1,6144,288]{1,2,0:T(8,128)(2,1)}, u32[]{:S(2)}) copy-start(bf16[1,6144,288]{1,2,0:T(8,128)(2,1)} %param.26) | copy-start | bytes 10616836
  228.4 65.7 %copy-start.12 = (f32[128,2]{0,1:T(2,128)S(1)}, f32[128,2]{0,1:T(2,128)}, u32[]{:S(2)}) copy-start(f32[128,2]{0,1:T(2,128)} %param.24) | copy-start | bytes 3076
  228.4 66.4 %copy-start.4 = (s32[256,1]{0,1:T(1,128)S(1)}, s32[256,1]{0,1:T(1,128)}, u32[]{:S(2)}) copy-start(s32[256,1]{0,1:T(1,128)} %copy-done.3) | copy-start | bytes 3076
  228.4 59.1 %reduce-scatter.5.cloned.1.call-start = ((), (), s32[]{:S(2)}) async-start(), calls=%async_computation.9 | async-start | bytes 2654208 | tf_op jit(solution)/shard_map/reduce_scatter | solution.py:68
  287.4 14.4 %all-to-all-start.3 = ((bf16[16,24,384]{2,1,0:T(8,128)(2,1)}), bf16[16,24,384]{2,1,0:T(8,128)(2,1)}, u32[]{:S(2)}, u32[]{:S(2)}) async-start(bf16[16,24,384]{2,1,0:T(8,128)(2,1)} %bitcast.199), calls=%async_computation.5 | async-start | bytes 589824 | tf_op jit(solution)/shard_map/all_to_all | solution.py:206
Sparse Core Ops, SparseCore 0:
  9.7 78.2 all-gather.5
  176.4 37.7 all-gather.7
  228.5 16.8 reduce-scatter.2
  247.8 39.5 reduce-scatter.4
where the time goes:
time: 321 us; the launch traced here: 316 us
  waiting for transfers between devices  148 us (46%)
  blocking collectives  55.5 us (17%)
  local copies, waits for them, and re-layouts  32.1 us (10%)
  other arithmetic  26.2 us (8%)
  matrix products  19.9 us (6%)
  starting transfers between devices  19.3 us (6%)
  between operations  15.3 us (5%)
    reduce_scatter x1, waiting for transfers between devices, summed_rows(): return lax.psum_scatter(tiles, chips, scatter_dimension=0, tiled=True)[0]  42 us
    all_gather x1, waiting for transfers between devices, shards(): lax.all_gather(lax.all_to_all(picked_rows.reshape(experts, capacity, moe_...  37.7 us
    all_gather x3, blocking collectives, carried_in(): lax.all_gather(part.astype(kind), axis)  32.5 us
    all_to_all x1, waiting for transfers between devices, sum_at_owner(): tiles = lax.all_to_all(cut_along(x, dim, peers), axis, 0, 0, tiled=True)  22.5 us
    reduce_scatter x1, waiting for transfers between devices, summed_rows(): tiles = lax.psum_scatter(tiles, core, scatter_dimension=0, tiled=True)  17 us
    all_gather x1, waiting for transfers between devices, shards(): lax.all_gather(out_weight, CTX, axis=1, tiled=True)  16.8 us
    all_to_all x1, blocking collectives, shards(): lax.all_to_all(picked_rows.reshape(experts, capacity, moe_input.shape[1])...  13.7 us
    unnamed x1, blocking collectives  9.26 us
  transfers between devices with their start and end apart: 7, of which 7 were waited for; matrix products, arithmetic and copies ran while one was open for 12% of the time, Pallas kernels for 0%

commit v1 on v0

v1 whole, which is shorter than its diff:
```python
import jax
import jax.numpy as jnp
from jax import lax
from jax.experimental import pallas as pl
from jax.experimental.pallas import tpu as pltpu
from jax.sharding import Mesh
from jax.sharding import PartitionSpec as P

D = 6144
HD = 128
CAP = 24
BLOCKS = 16
ROWS = 128
FEAT = 384
HID = 288
SLOTS = BLOCKS * CAP
CTX = ("ctx_0", "ctx_1")
TP = ("tp_0", "tp_1")
AXES = CTX + TP
ORDER = (4, 3, 5, 2, 6, 1, 7, 0)
BF = jnp.bfloat16
F32 = jnp.float32


def remote(src, dst, send_sem, recv_sem, to):
    return pltpu.make_async_remote_copy(
        src_ref=src,
        dst_ref=dst,
        send_sem=send_sem,
        recv_sem=recv_sem,
        device_id=to,
        device_id_type=pl.DeviceIdType.MESH,
    )


def place():
    return tuple(lax.axis_index(a) for a in AXES)


def partner_of(y, x, z, k):
    low = 2 * (z % 2) + k
    return low, (y, low, 2 * (z // 2) + x // 2, x % 2)


def greet(y, x, z, k):
    sem = pltpu.get_barrier_semaphore()
    for i in range(1, 16):
        c = (4 * y + x + i) % 16
        pl.semaphore_signal(
            sem, inc=1, device_id=(c // 4, c % 4, z, k), device_id_type=pl.DeviceIdType.MESH
        )
    for i in range(1, 16):
        t = (2 * z + k + i) % 16
        pl.semaphore_signal(
            sem, inc=1, device_id=(y, x, t // 2, t % 2), device_id_type=pl.DeviceIdType.MESH
        )
    low, partner = partner_of(y, x, z, k)

    @pl.when(low != x)
    def _():
        pl.semaphore_signal(sem, inc=1, device_id=partner, device_id_type=pl.DeviceIdType.MESH)

    pl.semaphore_wait(sem, 30 + ((low - x + 4) % 4 + 3) // 4)


class RingGather:
    def __init__(self, buf, ssem, rsem, me, device_at, half):
        self.buf, self.ssem, self.rsem = buf, ssem, rsem
        self.me, self.at, self.half = me, device_at, half

    def piece(self, member, part):
        return self.buf.at[member % 4, pl.ds(part * self.half, self.half)]

    def first(self, part, own):
        out = []
        for d, step in enumerate((1, -1)):
            cp = remote(
                own.at[pl.ds(part * self.half, self.half)],
                self.piece(self.me, part),
                self.ssem.at[d, part],
                self.rsem.at[d, part],
                self.at((self.me + step) % 4),
            )
            cp.start()
            out.append(cp)
        return out

    def arrived(self, d, part):
        step = (1, -1)[d]
        ref = self.piece(self.me + 4 - step, part)
        remote(
            ref, ref, self.ssem.at[d, part], self.rsem.at[d, part], self.at((self.me + step) % 4)
        ).wait_recv()

    def forward(self, d):
        step = (1, -1)[d]
        ref = self.piece(self.me + 4 - step, d)
        cp = remote(
            ref, ref, self.ssem.at[d, 2], self.rsem.at[d, 2], self.at((self.me + step) % 4)
        )
        cp.start()
        return cp

    def forwarded(self, d):
        step = (1, -1)[d]
        ref = self.piece(self.me + 2, d)
        remote(
            ref, ref, self.ssem.at[d, 2], self.rsem.at[d, 2], self.at((self.me + step) % 4)
        ).wait_recv()


class RingSum:
    def __init__(self, spot, rows, own, out, got, tbuf, rbuf, xs, xr, ssem, rsem):
        self.y, self.x, self.z, self.k = spot
        self.half = rows // 2
        self.own, self.out, self.got = own, out, got
        self.tbuf, self.rbuf = tbuf, rbuf
        self.xs, self.xr, self.ssem, self.rsem = xs, xr, ssem, rsem
        self.sent = []

    def swap(self, i):
        d = ORDER[i]
        cp = remote(
            self.out.at[i],
            self.got.at[i],
            self.xs.at[i],
            self.xr.at[i],
            (self.y, self.x, self.z, 1 - self.k),
        )
        cp.start()
        self.sent.append(cp)

    def swapped(self, i):
        remote(
            self.out.at[i],
            self.got.at[i],
            self.xs.at[i],
            self.xr.at[i],
            (self.y, self.x, self.z, 1 - self.k),
        ).wait_recv()

    def local(self, i, part):
        rows = pl.ds(part * self.half, self.half)
        return self.own[i, rows, :].astype(F32) + self.got[i, rows, :].astype(F32)

    def hop(self, d, s, part):
        to = (self.z + (1, 7)[d]) % 8
        return remote(
            self.tbuf.at[d, s, part],
            self.rbuf.at[d, s, part],
            self.ssem.at[d, s, part],
            self.rsem.at[d, s, part],
            (self.y, self.x, to, self.k),
        )

    def send(self, d, s, part, value):
        self.tbuf[d, s, part] = value.astype(BF)
        cp = self.hop(d, s, part)
        cp.start()
        self.sent.append(cp)

    def run(self, produce):
        produce(0)
        self.swap(0)
        produce(1)
        self.swap(1)
        produce(2)
        self.swap(2)
        self.swapped(0)
        self.send(0, 0, 0, self.local(0, 0))
        self.send(1, 0, 1, self.local(0, 1))
        self.swapped(1)
        self.send(0, 1, 1, self.local(1, 1))
        self.swapped(2)
        self.send(1, 1, 0, self.local(2, 0))
        for i in range(3, 8):
            produce(i)
            self.swap(i)
        self.hop(0, 0, 0).wait_recv()
        self.send(0, 1, 0, self.local(1, 0) + self.rbuf[0, 0, 0].astype(F32))
        self.hop(1, 0, 1).wait_recv()
        self.send(1, 1, 1, self.local(2, 1) + self.rbuf[1, 0, 1].astype(F32))
        for s in (2, 3):
            self.swapped(2 * s - 1)
            self.swapped(2 * s)
            for j in range(2):
                for d in range(2):
                    part = (1 - j) if d == 0 else j
                    self.hop(d, s - 1, part).wait_recv()
                    self.send(
                        d,
                        s,
                        part,
                        self.local(2 * s - 1 + d, part) + self.rbuf[d, s - 1, part].astype(F32),
                    )
        self.swapped(7)

    def result(self, part):
        self.hop(0, 3, part).wait_recv()
        self.hop(1, 3, part).wait_recv()
        return (
            self.local(7, part)
            + self.rbuf[0, 3, part].astype(F32)
            + self.rbuf[1, 3, part].astype(F32)
        )

    def finish(self):
        for cp in self.sent:
            cp.wait_send()


def mixer(
    rates, docs, q, k_in, v, again, w, res, mgain, ids,
    h_out, ids_out, gain_out,
    wbuf, hbuf, state, arrived, onward, incoming, resbuf, within,
    own, out, got, tbuf, rbuf,
    wss, wrs, hss, hrs, a1s, a1r, a2s, a2r, gs, gr, ps, pr, xs, xr, ts, tr, loc,
):
    spot = y, x, z, k = place()
    me, t = 4 * y + x, 2 * z + k
    low, partner = partner_of(*spot)
    sent = []
    greet(*spot)

    weights = RingGather(wbuf, wss, wrs, y, lambda i: (i, x, z, k), 256)
    heads = RingGather(hbuf, hss, hrs, x, lambda i: (y, i, z, k), 64)
    own_w = pltpu.make_async_copy(w, wbuf.at[y], loc.at[0])
    own_w.start()
    sent += weights.first(0, w)

    handed = [
        remote(res, resbuf, ps.at[0], pr.at[0], partner),
        remote(ids, ids_out, ps.at[1], pr.at[1], partner),
    ]
    kept = [
        pltpu.make_async_copy(res, resbuf, loc.at[1]),
        pltpu.make_async_copy(ids, ids_out, loc.at[2]),
    ]

    @pl.when(low != x)
    def _():
        for cp in handed:
            cp.start()

    @pl.when(low == x)
    def _():
        for cp in kept:
            cp.start()

    own_gain = pltpu.make_async_copy(mgain, gain_out.at[t], loc.at[3])
    own_gain.start()
    for i in range(1, 16):
        to = (t + i) % 16
        cp = remote(mgain, gain_out.at[t], gs.at[i], gr.at[i], (y, x, to // 2, to % 2))
        cp.start()
        sent.append(cp)

    start1 = docs[0]
    start2 = start1 + docs[1]
    start3 = start2 + docs[2]

    def seg(p):
        def past(s):
            return jnp.where(p >= s, 1, 0)

        base = jnp.where(p >= 0, 0, -1)
        return base + past(start1) + past(start2) + past(start3)

    first = me * ROWS
    last_seg = seg(first + ROWS - 1)
    before = seg(first - 1)
    row = lax.broadcasted_iota(jnp.int32, (ROWS, HD), 0)
    col = lax.broadcasted_iota(jnp.int32, (ROWS, HD), 1)
    seg_row, seg_col = seg(first + row), seg(first + col)
    rowf = row.astype(F32)
    at_end = jnp.where(seg_row == last_seg, 1.0, 0.0)
    for h in range(4):
        rate = rates[4 * t + h]
        cols = slice(h * HD, (h + 1) * HD)
        fading = at_end * jnp.exp(-rate * (ROWS - 1.0 - rowf))
        faded = (k_in[:, cols].astype(F32) * fading).astype(BF)
        state[h * HD : (h + 1) * HD, :] = lax.dot_general(
            faded, v[:, cols], (((0,), (0,)), ((), ())), preferred_element_type=F32
        ).astype(BF)

    own_state = pltpu.make_async_copy(
        state.at[pl.ds(pl.multiple_of(me * 32, 32), 32)], arrived.at[me], loc.at[4]
    )
    own_state.start()
    for i in range(1, 16):
        to = (me + i) % 16
        cp = remote(
            state.at[pl.ds(pl.multiple_of(to * 32, 32), 32)],
            arrived.at[me],
            a1s.at[i],
            a1r.at[i],
            (to // 4, to % 4, z, k),
        )
        cp.start()
        sent.append(cp)
    sent += weights.first(1, w)

    allowed = jnp.where((row >= col) & (seg_row == seg_col), 1.0, 0.0)
    gap = jnp.maximum(row - col, 0).astype(F32)
    for h in range(4):
        rate = rates[4 * t + h]
        cols = slice(h * HD, (h + 1) * HD)
        scores = lax.dot_general(
            q[:, cols], k_in[:, cols], (((1,), (1,)), ((), ())), preferred_element_type=F32
        )
        mixed = (scores * (allowed * jnp.exp(-rate * gap))).astype(BF)
        within[:, cols] = jnp.dot(mixed, v[:, cols], preferred_element_type=F32)

    own_state.wait()
    for i in range(1, 16):
        ref = arrived.at[(me - i + 16) % 16]
        remote(ref, ref, a1s.at[i], a1r.at[i], (y, x, z, 1 - k)).wait_recv()
    decay = jnp.exp(jnp.zeros((32, HD), F32) - rates[4 * t + y] * ROWS)
    running = jnp.zeros((32, HD), F32)
    for b in range(BLOCKS):
        onward[b] = running.astype(BF)
        same = seg(jnp.int32(b * ROWS + ROWS - 1)) == seg(jnp.int32(b * ROWS - 1))
        running = running * (decay * jnp.where(same, 1.0, 0.0)) + arrived[b].astype(F32)
    own_onward = pltpu.make_async_copy(onward.at[me], incoming.at[me], loc.at[5])
    own_onward.start()
    for i in range(1, 16):
        to = (me + i) % 16
        cp = remote(
            onward.at[to], incoming.at[me], a2s.at[i], a2r.at[i], (to // 4, to % 4, z, k)
        )
        cp.start()
        sent.append(cp)
    for d in range(2):
        for part in range(2):
            weights.arrived(d, part)
    for d in range(2):
        sent.append(weights.forward(d))
    own_onward.wait()
    for i in range(1, 16):
        ref = incoming.at[(me - i + 16) % 16]
        remote(ref, ref, a2s.at[i], a2r.at[i], (y, x, z, 1 - k)).wait_recv()

    reached = jnp.where(seg_row == before, 1.0, 0.0)
    for h in range(4):
        rate = rates[4 * t + h]
        cols = slice(h * HD, (h + 1) * HD)
        inc = incoming[4 * h : 4 * h + 4].reshape(HD, HD)
        inter = jnp.dot(q[:, cols], inc, preferred_element_type=F32)
        both = within[:, cols] + inter * (reached * jnp.exp(-rate * (rowf + 1.0)))
        scale = lax.rsqrt(jnp.mean(both * both, axis=1, keepdims=True) + 1e-06)
        within[:, cols] = both * scale * again[:, cols]
    hbuf[x] = within[...].astype(BF)
    sent += heads.first(0, hbuf.at[x])
    sent += heads.first(1, hbuf.at[x])
    heads.arrived(0, 0)
    sent.append(heads.forward(0))
    heads.arrived(1, 1)
    sent.append(heads.forward(1))
    heads.arrived(0, 1)
    heads.arrived(1, 0)
    own_w.wait()
    for d in range(2):
        weights.forwarded(d)
    for d in range(2):
        heads.forwarded(d)

    total = RingSum(spot, ROWS, own, out, got, tbuf, rbuf, xs, xr, ts, tr)

    def produce(i):
        chunk = (z + ORDER[i]) % 8
        pair = 2 * (chunk % 2)
        wide = wbuf[chunk // 2]
        out[i] = jnp.dot(hbuf[pair + 1 - k], wide, preferred_element_type=F32).astype(BF)
        own[i] = jnp.dot(hbuf[pair + k], wide, preferred_element_type=F32).astype(BF)

    total.run(produce)

    @pl.when(low != x)
    def _():
        for cp in handed:
            cp.wait()

    @pl.when(low == x)
    def _():
        for cp in kept:
            cp.wait()

    for part in range(2):
        rows = slice(part * 64, part * 64 + 64)
        h_out[rows, :] = (resbuf[rows, :].astype(F32) + total.result(part)).astype(BF)
    own_gain.wait()
    for i in range(1, 16):
        ref = gain_out.at[(t - i + 16) % 16]
        remote(ref, ref, gs.at[i], gr.at[i], (y, x, z, 1 - k)).wait_recv()
    for cp in sent:
        cp.wait_send()
    total.finish()


def slot_hits(ids):
    expert = lax.broadcasted_iota(jnp.int32, (BLOCKS, CAP, ROWS), 0).reshape(SLOTS, ROWS)
    place_in = lax.broadcasted_iota(jnp.int32, (BLOCKS, CAP, ROWS), 1).reshape(SLOTS, ROWS)
    hit0 = expert == ids[0:1, :]
    hit1 = expert == ids[1:2, :]
    named = jnp.where(hit0 | hit1, 1.0, 0.0)
    earlier = lax.broadcasted_iota(jnp.int32, (ROWS, ROWS), 0)
    later = lax.broadcasted_iota(jnp.int32, (ROWS, ROWS), 1)
    rank = jnp.dot(
        named.astype(BF),
        jnp.where(earlier < later, 1.0, 0.0).astype(BF),
        preferred_element_type=F32,
    )
    here = rank == place_in.astype(F32)
    return hit0 & here, hit1 & here


def experts(
    h, ids_p, gains, ids_n, wts, wg_hbm, wu_hbm, wd_hbm,
    o_ref,
    wgu, wd, ds, xb, lhs, acc, squares, act, hn, qs, rb,
    own, out, got, tbuf, rbuf,
    dss, dsr, fs, fr, cs, cr, qss, qsr, ps, pr, xs, xr, ts, tr, loc,
):
    spot = y, x, z, k = place()
    me, t = 4 * y + x, 2 * z + k
    low, partner = partner_of(*spot)
    peer = (y, x, z, 1 - k)
    sent = []
    loads = [
        pltpu.make_async_copy(wg_hbm, wgu.at[pl.ds(0, HID)], loc.at[0]),
        pltpu.make_async_copy(wu_hbm, wgu.at[pl.ds(FEAT, HID)], loc.at[1]),
        pltpu.make_async_copy(wd_hbm, wd, loc.at[2]),
    ]
    for cp in loads:
        cp.start()

    hit0, hit1 = slot_hits(ids_p)
    pick = jnp.where(hit0 | hit1, 1.0, 0.0).astype(BF)
    picked = jnp.dot(pick, h[...], preferred_element_type=F32)
    ds[...] = picked.reshape(BLOCKS, CAP, FEAT).astype(BF)
    greet(*spot)

    mine = 4 * x + y
    own_rows = pltpu.make_async_copy(ds.at[me], xb.at[t, mine], loc.at[3])
    own_rows.start()
    for i in range(1, 16):
        to = (me + i) % 16
        cp = remote(ds.at[to], xb.at[t, mine], dss.at[i], dsr.at[i], (to // 4, to % 4, z, k))
        cp.start()
        sent.append(cp)
    handed = remote(h, hn, ps.at[0], pr.at[0], partner)
    kept = pltpu.make_async_copy(h, hn, loc.at[4])

    @pl.when(low != x)
    def _():
        handed.start()

    @pl.when(low == x)
    def _():
        kept.start()

    own_rows.wait()
    for i in range(1, 16):
        c = (me - i + 16) % 16
        ref = xb.at[t, 4 * (c % 4) + c // 4]
        remote(ref, ref, dss.at[i], dsr.at[i], peer).wait_recv()

    def half(zz, kk, part):
        return xb.at[2 * ((zz + 8) % 8) + kk, pl.ds(part * 8, 8)]

    def ring(d, s, part, ref):
        to = (z + (1, 7)[d]) % 8
        return remote(ref, ref, fs.at[d, s, part], fr.at[d, s, part], (y, x, to, k))

    def over(slot, part, ref):
        return remote(ref, ref, cs.at[slot, part], cr.at[slot, part], peer)

    def push(cp):
        cp.start()
        sent.append(cp)

    def crossed(slot, dist):
        for part in range(2):
            over(slot, part, half(z + dist, 1 - k, part)).wait_recv()

    for part in range(2):
        ref = half(z, k, part)
        push(ring(0, 0, part, ref))
        push(ring(1, 0, part, ref))
        push(over(0, part, ref))

    wgu[HID:FEAT, :] = jnp.zeros((FEAT - HID, D), BF)
    acc[...] = jnp.zeros_like(acc)
    squares[...] = jnp.zeros_like(squares)

    def multiply(group):
        for xx in range(4):
            gain = gains[4 * group + xx]
            for xp in range(4):
                rows = slice(96 * xp, 96 * xp + 96)
                piece = xb[4 * group + xp, 4 * xx : 4 * xx + 4].astype(F32).reshape(96, FEAT)
                sq = piece * piece
                squares[rows, :] += sq[:, 0:128] + sq[:, 128:256] + sq[:, 256:384]
                lhs[rows, xx * FEAT : (xx + 1) * FEAT] = (piece * gain).astype(BF)
        cols = pl.ds(pl.multiple_of(group * 1536, 1536), 1536)
        acc[...] += lax.dot_general(
            lhs[...], wgu[:, cols], (((1,), (1,)), ((), ())), preferred_element_type=F32
        )

    side = jnp.where(z % 2 == 0, 3, 1)
    pair = z // 2
    for s in (1, 2, 3):
        for part in range(2):
            for d in range(2):
                behind = -s if d == 0 else s
                ref = half(z + behind, k, part)
                ring(d, s - 1, part, ref).wait_recv()
                if s < 3 or part == d:
                    push(ring(d, s, part, ref))
                push(over(2 * s - 1 + d, part, ref))
        if s == 1:
            crossed(0, 0)
            crossed(1, -1)
            crossed(2, 1)
            loads[0].wait()
            loads[1].wait()
            multiply(pair)
        elif s == 2:
            crossed(3, -2)
            crossed(4, 2)
            multiply((pair + side) % 4)
        else:
            crossed(5, -3)
            crossed(6, 3)
            multiply((pair + 4 - side) % 4)
    for d in range(2):
        ref = half(z + 4, k, d)
        ring(d, 3, d, ref).wait_recv()
        push(over(7, d, ref))
    crossed(7, 4)
    multiply((pair + 2) % 4)

    total_sq = jnp.sum(squares[...], axis=1, keepdims=True)
    scale = lax.rsqrt(total_sq / D + 1e-05)
    gate = acc[:, :HID] * scale
    lifted = acc[:, FEAT:] * scale
    act[...] = (gate / (1.0 + jnp.exp(-gate)) * lifted).astype(BF)
    loads[2].wait()

    total = RingSum(spot, SLOTS, own, out, got, tbuf, rbuf, xs, xr, ts, tr)

    def produce(i):
        chunk = (z + ORDER[i]) % 8

        def tile(lane):
            cols = pl.ds(pl.multiple_of((2 * chunk + lane) * FEAT, FEAT), FEAT)
            return jnp.dot(act[...], wd[:, cols], preferred_element_type=F32).astype(BF)

        out[i] = tile(1 - k)
        own[i] = tile(k)

    total.run(produce)
    for part in range(2):
        qs[part * 8 : part * 8 + 8] = total.result(part).reshape(8, CAP, FEAT).astype(BF)
    own_back = pltpu.make_async_copy(qs.at[mine], rb.at[me], loc.at[5])
    own_back.start()
    for i in range(1, 16):
        to = (me + i) % 16
        push(
            remote(
                qs.at[4 * (to % 4) + to // 4],
                rb.at[me],
                qss.at[i],
                qsr.at[i],
                (to // 4, to % 4, z, k),
            )
        )
    hit0, hit1 = slot_hits(ids_n)
    part_of = jnp.where(hit0, wts[0:1, :], 0.0) + jnp.where(hit1, wts[1:2, :], 0.0)
    coarse = part_of.astype(BF)
    fine = (part_of - coarse.astype(F32)).astype(BF)

    @pl.when(low != x)
    def _():
        handed.wait()

    @pl.when(low == x)
    def _():
        kept.wait()

    own_back.wait()
    for i in range(1, 16):
        ref = rb.at[(me - i + 16) % 16]
        remote(ref, ref, qss.at[i], qsr.at[i], peer).wait_recv()
    back = rb[...].astype(F32).reshape(SLOTS, FEAT).astype(BF)
    dims = (((0,), (0,)), ((), ()))
    mixture = lax.dot_general(coarse, back, dims, preferred_element_type=F32)
    mixture += lax.dot_general(fine, back, dims, preferred_element_type=F32)
    o_ref[...] = (hn[...].astype(F32) + mixture).astype(BF)
    for cp in sent:
        cp.wait_send()
    total.finish()


def dma(*shape):
    return pltpu.SemaphoreType.DMA(shape)


def ring_scratch(rows):
    half = rows // 2
    return [
        pltpu.VMEM((8, rows, FEAT), BF),
        pltpu.VMEM((8, rows, FEAT), BF),
        pltpu.VMEM((8, rows, FEAT), BF),
        pltpu.VMEM((2, 4, 2, half, FEAT), BF),
        pltpu.VMEM((2, 4, 2, half, FEAT), BF),
    ]


VM = pl.BlockSpec(memory_space=pltpu.VMEM)
SM = pl.BlockSpec(memory_space=pltpu.SMEM)
ANY = pl.BlockSpec(memory_space=pl.ANY)


def shards(
    residual, query_rows, key_rows, value_rows, head_rates, doc_lengths, attn_gain, out_weight,
    moe_gain, expert_ids, expert_weights, gate_weight, up_weight, down_weight,
):
    ids = expert_ids.T
    h, ids_p, gains = pl.pallas_call(
        mixer,
        out_shape=(
            jax.ShapeDtypeStruct((ROWS, FEAT), BF),
            jax.ShapeDtypeStruct((2, ROWS), jnp.int32),
            jax.ShapeDtypeStruct((16, 1, FEAT), F32),
        ),
        in_specs=[SM, SM] + [VM] * 8,
        out_specs=(VM, VM, VM),
        scratch_shapes=[
            pltpu.VMEM((4, 512, FEAT), BF),
            pltpu.VMEM((4, ROWS, 512), BF),
            pltpu.VMEM((512, HD), BF),
            pltpu.VMEM((16, 32, HD), BF),
            pltpu.VMEM((16, 32, HD), BF),
            pltpu.VMEM((16, 32, HD), BF),
            pltpu.VMEM((ROWS, FEAT), BF),
            pltpu.VMEM((ROWS, 512), F32),
            *ring_scratch(ROWS),
            dma(2, 3), dma(2, 3), dma(2, 3), dma(2, 3),
            dma(16), dma(16), dma(16), dma(16), dma(16), dma(16),
            dma(2), dma(2), dma(8), dma(8), dma(2, 4, 2), dma(2, 4, 2), dma(6),
        ],
        compiler_params=pltpu.CompilerParams(
            collective_id=0, has_side_effects=True, vmem_limit_bytes=40 << 20
        ),
        name="mixer",
    )(
        head_rates, doc_lengths, query_rows, key_rows, value_rows, attn_gain.reshape(1, -1),
        out_weight, residual, moe_gain.reshape(1, -1), ids,
    )
    return pl.pallas_call(
        experts,
        out_shape=jax.ShapeDtypeStruct((ROWS, FEAT), BF),
        in_specs=[VM] * 5 + [ANY] * 3,
        out_specs=VM,
        scratch_shapes=[
            pltpu.VMEM((FEAT + HID, D), BF),
            pltpu.VMEM((HID, D), BF),
            pltpu.VMEM((BLOCKS, CAP, FEAT), BF),
            pltpu.VMEM((16, BLOCKS, CAP, FEAT), BF),
            pltpu.VMEM((SLOTS, 4 * FEAT), BF),
            pltpu.VMEM((SLOTS, FEAT + HID), F32),
            pltpu.VMEM((SLOTS, 128), F32),
            pltpu.VMEM((SLOTS, HID), BF),
            pltpu.VMEM((ROWS, FEAT), BF),
            pltpu.VMEM((BLOCKS, CAP, FEAT), BF),
            pltpu.VMEM((BLOCKS, CAP, FEAT), BF),
            *ring_scratch(SLOTS),
            dma(16), dma(16), dma(2, 4, 2), dma(2, 4, 2), dma(8, 2), dma(8, 2),
            dma(16), dma(16), dma(1), dma(1), dma(8), dma(8), dma(2, 4, 2), dma(2, 4, 2), dma(6),
        ],
        compiler_params=pltpu.CompilerParams(
            collective_id=1, has_side_effects=True, vmem_limit_bytes=60 << 20
        ),
        name="experts",
    )(
        h, ids_p, gains, ids, expert_weights.T,
        gate_weight[0].T, up_weight[0].T, down_weight[0],
    )


def solution(mesh):
    finer = Mesh(mesh.devices.reshape(4, 4, 8, 2), AXES)
    placed = (
        P(CTX, TP), P(CTX, TP), P(CTX, TP), P(CTX, TP), P(), P(), P(TP), P(TP, CTX), P(TP),
        P(CTX, None), P(CTX, None), P(CTX, None, TP), P(CTX, None, TP), P(CTX, TP, None),
    )
    return jax.shard_map(shards, mesh=finer, in_specs=placed, out_specs=P(CTX, TP), check_vma=False)
```

time: 321 us -> 139 us (0.43); the launches traced: 316 us -> 138 us
  waiting for transfers between devices: 148 us -> 0 us
  Pallas kernels: 0 us -> 126 us
  blocking collectives: 55.5 us -> 0 us
  other arithmetic: 26.2 us -> 0 us
  local copies, waits for them, and re-layouts: 32.1 us -> 11.3 us
  matrix products: 19.9 us -> 0 us
  starting transfers between devices: 19.3 us -> 0 us
  between operations: 15.3 us -> 0.04 us
    pallas_call x0 -> x2, Pallas kernels: none -> 126 us  [the longest x1 78.4 us: shards(): pl.pallas_call(experts, out_shape=jax.ShapeDtypeStruct((ROWS, FEAT), BF),...]
    reduce_scatter x2 -> x0, waiting for transfers between devices: 59 us -> none  [the longest x1 42 us: summed_rows(): return lax.psum_scatter(tiles, chips, scatter_dimension=0, tiled=True)[0]]
    all_gather x2 -> x0, waiting for transfers between devices: 54.5 us -> none  [the longest x1 37.7 us: shards(): lax.all_gather(lax.all_to_all(picked_rows.reshape(experts, capacity, moe_...]
    all_to_all x3 -> x0, waiting for transfers between devices: 33.7 us -> none  [the longest x1 22.5 us: sum_at_owner(): tiles = lax.all_to_all(cut_along(x, dim, peers), axis, 0, 0, tiled=True)]
    all_gather x3 -> x0, blocking collectives: 32.5 us -> none  [carried_in(): lax.all_gather(part.astype(kind), axis)]
    dot_general x7 -> x0, matrix products: 19.9 us -> none  [the longest x1 5.57 us: shards(): jnp.dot(flat_in, gate_weight[0], preferred_element_type=jnp.float32)]
    all_to_all x3 -> x0, starting transfers between devices: 19 us -> none  [the longest x1 8.3 us: sum_at_owner(): tiles = lax.all_to_all(cut_along(x, dim, peers), axis, 0, 0, tiled=True)]
    all_to_all x1 -> x0, blocking collectives: 13.7 us -> none  [shards(): lax.all_to_all(picked_rows.reshape(experts, capacity, moe_input.shape[1])...]
  transfers between devices with their start and end apart: 7 -> 0, of which waited for: 7 -> 0; matrix products, arithmetic and copies ran while one was open for 12% -> 0% of each run, Pallas kernels for 0% -> 0%
where the time goes in v1:
time: 139 us; the launch traced here: 138 us
  Pallas kernels  126 us (91%)
  local copies, waits for them, and re-layouts  11.3 us (8%)
    pallas_call x1, Pallas kernels, shards(): pl.pallas_call(experts, out_shape=jax.ShapeDtypeStruct((ROWS, FEAT), BF),...  78.4 us
    pallas_call x1, Pallas kernels, shards(): pl.pallas_call(mixer, out_shape=(jax.ShapeDtypeStruct((ROWS, FEAT), BF),...  48 us
    unnamed x25, local copies, waits for them, and re-layouts  10.6 us

profile of v1, /device:TPU:1, one launch (start us, length us, event | category | flops | bytes accessed | tf_op | source)
XLA Modules:
  0.0 137.8 jit_solution(12074444544856999420)
XLA Ops:
  0.0 0.7 reshape.7.mgain
  0.7 0.0 copy-start
  0.7 1.0 copy-done
  1.7 0.0 copy-start.1
  1.7 0.9 copy-done.1
  2.6 0.0 copy-start.2
  2.6 0.9 copy-done.2
  3.5 0.0 copy-start.3
  3.5 0.9 copy-done.3
  4.4 0.0 copy-start.5
  4.4 0.9 copy-done.5
  5.3 0.0 copy-start.7
  5.3 0.7 copy-done.7
  6.0 0.0 copy-start.8
  6.0 0.7 copy-done.8
  6.7 0.7 copy-done.10
  7.3 0.7 copy-done.11
  8.0 48.0 %mixer.1 = (bf16[128,384]{1,0:T(8,128)(2,1)S(1)}, s32[2,128]{1,0:T(2,128)S(1)}, f32[16,1,384]{2,1,0:T(1,128)S(1)}) custom-call(f32[64]{0:T(128)S(1)} %copy-done.10, s32[4]{0:T(128)S(1)} %copy-done.11, bf16[128,512]{1,0:T(8,128)(2,1)S(1)} %copy-done.1, bf16[128,512]{1,0:T(8,128)(2,1)S(1)} %copy-done.2, bf16[128,512]{1,0:T(8,128)(2,1)S(1)} %copy-done.3, ...), custom_call_target="tpu_custom_call" | custom-call | tf_op jit(solution)/shard_map/mixer/pallas_call | solution.py:630
  56.0 0.0 copy-start.4
  56.0 0.6 copy-done.4
  56.7 0.6 copy-done.6
  57.3 0.6 copy-done.9
  57.8 78.4 %experts.1 = bf16[128,384]{1,0:T(8,128)(2,1)} custom-call(bf16[128,384]{1,0:T(8,128)(2,1)} %copy-done.4, s32[2,128]{1,0:T(2,128)} %copy-done.9, f32[16,1,384]{2,1,0:T(1,128)} %copy-done.6, s32[2,128]{1,0:T(2,128)} %bitcast.10, f32[2,128]{1,0:T(2,128)} %bitcast.16, bf16[288,6144]{1,0:T(8,128)(2,1)} %bitcast.13, bf16[288,6144]{1,0:T(8,128)(2,1)} %bitcast.14, ...), custom_call_target="tpu_custom_call" | custom-call | tf_op jit(solution)/shard_map/experts/pallas_call | solution.py:661
  136.2 1.5 %copy.16 = bf16[128,384]{1,0:T(8,128)(2,1)} copy(bf16[128,384]{1,0:T(8,128)(2,1)} %experts.1) | data formatting | bytes 196608
  (4 shorter events, 0.0 us)
Async XLA Ops:
  0.7 1.0 copy-start
  1.7 0.9 copy-start.1
  2.6 0.9 copy-start.2
  3.5 0.9 copy-start.3
  4.4 0.9 copy-start.5
  5.3 0.7 copy-start.7
  6.0 0.7 copy-start.8
  6.6 0.7 copy-start.10
  7.3 0.7 copy-start.11
  56.0 0.6 copy-start.4
  56.6 0.6 copy-start.6
  57.3 0.6 copy-start.9

commit v2 on v1

--- a/solution.py
+++ b/solution.py
@@ -204,22 +204,30 @@
             + self.rbuf[1, 3, part].astype(F32)
         )
 
-    def finish(self):
-        for cp in self.sent:
-            cp.wait_send()
-
 
 def mixer(
-    rates, docs, q, k_in, v, again, w, res, mgain, ids,
-    h_out, ids_out, gain_out,
+    rates_hbm, docs_hbm, q_hbm, k_hbm, v_hbm, again_hbm, w, res, mgain, ids,
+    rates, docs, q, k_in, v, again,
+    h_out, ids_all, gain_out,
     wbuf, hbuf, state, arrived, onward, incoming, resbuf, within,
     own, out, got, tbuf, rbuf,
-    wss, wrs, hss, hrs, a1s, a1r, a2s, a2r, gs, gr, ps, pr, xs, xr, ts, tr, loc,
+    wss, wrs, hss, hrs, a1s, a1r, a2s, a2r, gs, gr, ps, pr, ids_s, ids_r, xs, xr, ts, tr, loc, start_weights,
 ):
     spot = y, x, z, k = place()
     me, t = 4 * y + x, 2 * z + k
     low, partner = partner_of(*spot)
     sent = []
+    loads = [
+        pltpu.make_async_copy(a, b, loc.at[6 + i])
+        for i, (a, b) in enumerate(
+            (
+                (k_hbm, k_in), (v_hbm, v), (rates_hbm, rates), (docs_hbm, docs), (q_hbm, q),
+                (again_hbm, again),
+            )
+        )
+    ]
+    for cp in loads:
+        cp.start()
     greet(*spot)
 
     weights = RingGather(wbuf, wss, wrs, y, lambda i: (i, x, z, k), 256)
@@ -228,33 +236,35 @@
     own_w.start()
     sent += weights.first(0, w)
 
-    handed = [
-        remote(res, resbuf, ps.at[0], pr.at[0], partner),
-        remote(ids, ids_out, ps.at[1], pr.at[1], partner),
-    ]
-    kept = [
-        pltpu.make_async_copy(res, resbuf, loc.at[1]),
-        pltpu.make_async_copy(ids, ids_out, loc.at[2]),
-    ]
+    handed = remote(res, resbuf, ps.at[0], pr.at[0], partner)
+    kept = pltpu.make_async_copy(res, resbuf, loc.at[1])
 
     @pl.when(low != x)
     def _():
-        for cp in handed:
-            cp.start()
+        handed.start()
 
     @pl.when(low == x)
     def _():
-        for cp in kept:
-            cp.start()
-
-    own_gain = pltpu.make_async_copy(mgain, gain_out.at[t], loc.at[3])
+        kept.start()
+
+    own_ids = pltpu.make_async_copy(ids, ids_all.at[x], loc.at[2])
+    own_ids.start()
+    for i in range(1, 4):
+        cp = remote(ids, ids_all.at[x], ids_s.at[i], ids_r.at[i], (y, (x + i) % 4, z, k))
+        cp.start()
+        sent.append(cp)
+
+    own_gain = pltpu.make_async_copy(mgain, gain_out.at[t, 0], loc.at[3])
     own_gain.start()
     for i in range(1, 16):
         to = (t + i) % 16
-        cp = remote(mgain, gain_out.at[t], gs.at[i], gr.at[i], (y, x, to // 2, to % 2))
+        cp = remote(mgain, gain_out.at[t, 0], gs.at[i], gr.at[i], (y, x, to // 2, to % 2))
         cp.start()
         sent.append(cp)
 
+    start_weights()
+    for cp in loads[:4]:
+        cp.wait()
     start1 = docs[0]
     start2 = start1 + docs[1]
     start3 = start2 + docs[2]
@@ -300,6 +310,8 @@
         sent.append(cp)
     sent += weights.first(1, w)
 
+    loads[4].wait()
+    loads[5].wait()
     allowed = jnp.where((row >= col) & (seg_row == seg_col), 1.0, 0.0)
     gap = jnp.maximum(row - col, 0).astype(F32)
     for h in range(4):
@@ -377,24 +389,24 @@
 
     @pl.when(low != x)
     def _():
-        for cp in handed:
-            cp.wait()
+        handed.wait()
 
     @pl.when(low == x)
     def _():
-        for cp in kept:
-            cp.wait()
+        kept.wait()
 
     for part in range(2):
         rows = slice(part * 64, part * 64 + 64)
         h_out[rows, :] = (resbuf[rows, :].astype(F32) + total.result(part)).astype(BF)
     own_gain.wait()
     for i in range(1, 16):
-        ref = gain_out.at[(t - i + 16) % 16]
+        ref = gain_out.at[(t - i + 16) % 16, 0]
         remote(ref, ref, gs.at[i], gr.at[i], (y, x, z, 1 - k)).wait_recv()
-    for cp in sent:
-        cp.wait_send()
-    total.finish()
+    own_ids.wait()
+    for i in range(1, 4):
+        ref = ids_all.at[(x - i + 4) % 4]
+        remote(ref, ref, ids_s.at[i], ids_r.at[i], (y, x, z, 1 - k)).wait_recv()
+    return sent + total.sent
 
 
 def slot_hits(ids):
@@ -415,9 +427,9 @@
 
 
 def experts(
-    h, ids_p, gains, ids_n, wts, wg_hbm, wu_hbm, wd_hbm,
+    wts, wgu, wd, weight_loads, h, ids_all, gains,
     o_ref,
-    wgu, wd, ds, xb, lhs, acc, squares, act, hn, qs, rb,
+    ds, xb, lhs, acc, squares, act, hn, qs, rb,
     own, out, got, tbuf, rbuf,
     dss, dsr, fs, fr, cs, cr, qss, qsr, ps, pr, xs, xr, ts, tr, loc,
 ):
@@ -426,19 +438,10 @@
     low, partner = partner_of(*spot)
     peer = (y, x, z, 1 - k)
     sent = []
-    loads = [
-        pltpu.make_async_copy(wg_hbm, wgu.at[pl.ds(0, HID)], loc.at[0]),
-        pltpu.make_async_copy(wu_hbm, wgu.at[pl.ds(FEAT, HID)], loc.at[1]),
-        pltpu.make_async_copy(wd_hbm, wd, loc.at[2]),
-    ]
-    for cp in loads:
-        cp.start()
-
-    hit0, hit1 = slot_hits(ids_p)
+    hit0, hit1 = slot_hits(ids_all[low])
     pick = jnp.where(hit0 | hit1, 1.0, 0.0).astype(BF)
     picked = jnp.dot(pick, h[...], preferred_element_type=F32)
     ds[...] = picked.reshape(BLOCKS, CAP, FEAT).astype(BF)
-    greet(*spot)
 
     mine = 4 * x + y
     own_rows = pltpu.make_async_copy(ds.at[me], xb.at[t, mine], loc.at[3])
@@ -522,8 +525,8 @@
             crossed(0, 0)
             crossed(1, -1)
             crossed(2, 1)
-            loads[0].wait()
-            loads[1].wait()
+            weight_loads[0].wait()
+            weight_loads[1].wait()
             multiply(pair)
         elif s == 2:
             crossed(3, -2)
@@ -545,7 +548,7 @@
     gate = acc[:, :HID] * scale
     lifted = acc[:, FEAT:] * scale
     act[...] = (gate / (1.0 + jnp.exp(-gate)) * lifted).astype(BF)
-    loads[2].wait()
+    weight_loads[2].wait()
 
     total = RingSum(spot, SLOTS, own, out, got, tbuf, rbuf, xs, xr, ts, tr)
 
@@ -575,7 +578,8 @@
                 (to // 4, to % 4, z, k),
             )
         )
-    hit0, hit1 = slot_hits(ids_n)
+    weight_loads[3].wait()
+    hit0, hit1 = slot_hits(ids_all[x])
     part_of = jnp.where(hit0, wts[0:1, :], 0.0) + jnp.where(hit1, wts[1:2, :], 0.0)
     coarse = part_of.astype(BF)
     fine = (part_of - coarse.astype(F32)).astype(BF)
@@ -597,9 +601,46 @@
     mixture = lax.dot_general(coarse, back, dims, preferred_element_type=F32)
     mixture += lax.dot_general(fine, back, dims, preferred_element_type=F32)
     o_ref[...] = (hn[...].astype(F32) + mixture).astype(BF)
+    return sent + total.sent
+
+
+def layer(*refs):
+    ins, o_ref, refs = refs[:14], refs[14], list(refs[15:])
+
+    def take(n):
+        taken = refs[:n]
+        del refs[:n]
+        return taken
+
+    wg_hbm, wu_hbm, wd_hbm, wts_hbm = ins[10:]
+    wgu, wd, wts, weight_sems = take(4)
+    early = take(6)
+    passed = h, ids_all, gains = take(3)
+    mix_scratch = take(8)
+    mix_ring = take(5)
+    mix_sems = take(19)
+    moe_scratch = take(9)
+    moe_ring = take(5)
+    moe_sems = take(15)
+    weight_loads = [
+        pltpu.make_async_copy(wg_hbm, wgu.at[pl.ds(0, HID)], weight_sems.at[0]),
+        pltpu.make_async_copy(wu_hbm, wgu.at[pl.ds(FEAT, HID)], weight_sems.at[1]),
+        pltpu.make_async_copy(wd_hbm, wd, weight_sems.at[2]),
+        pltpu.make_async_copy(wts_hbm, wts, weight_sems.at[3]),
+    ]
+
+    def start_weights():
+        for cp in weight_loads:
+            cp.start()
+
+    sent = mixer(
+        *ins[:10], *early, *passed, *mix_scratch, *mix_ring, *mix_sems, start_weights
+    )
+    sent += experts(
+        wts, wgu, wd, weight_loads, *passed, o_ref, *moe_scratch, *moe_ring, *moe_sems
+    )
     for cp in sent:
         cp.wait_send()
-    total.finish()
 
 
 def dma(*shape):
@@ -617,8 +658,6 @@
     ]
 
 
-VM = pl.BlockSpec(memory_space=pltpu.VMEM)
-SM = pl.BlockSpec(memory_space=pltpu.SMEM)
 ANY = pl.BlockSpec(memory_space=pl.ANY)
 
 
@@ -626,17 +665,25 @@
     residual, query_rows, key_rows, value_rows, head_rates, doc_lengths, attn_gain, out_weight,
     moe_gain, expert_ids, expert_weights, gate_weight, up_weight, down_weight,
 ):
-    ids = expert_ids.T
-    h, ids_p, gains = pl.pallas_call(
-        mixer,
-        out_shape=(
-            jax.ShapeDtypeStruct((ROWS, FEAT), BF),
-            jax.ShapeDtypeStruct((2, ROWS), jnp.int32),
-            jax.ShapeDtypeStruct((16, 1, FEAT), F32),
-        ),
-        in_specs=[SM, SM] + [VM] * 8,
-        out_specs=(VM, VM, VM),
+    return pl.pallas_call(
+        layer,
+        out_shape=jax.ShapeDtypeStruct((ROWS, FEAT), BF),
+        in_specs=[ANY] * 14,
+        out_specs=pl.BlockSpec(memory_space=pltpu.VMEM),
         scratch_shapes=[
+            pltpu.VMEM((FEAT + HID, D), BF),
+            pltpu.VMEM((HID, D), BF),
+            pltpu.VMEM((2, ROWS), F32),
+            dma(4),
+            pltpu.SMEM((64,), F32),
+            pltpu.SMEM((4,), jnp.int32),
+            pltpu.VMEM((ROWS, 512), BF),
+            pltpu.VMEM((ROWS, 512), BF),
+            pltpu.VMEM((ROWS, 512), BF),
+            pltpu.VMEM((1, 512), F32),
+            pltpu.VMEM((ROWS, FEAT), BF),
+            pltpu.VMEM((4, 2, ROWS), jnp.int32),
+            pltpu.VMEM((16, 1, FEAT), F32),
             pltpu.VMEM((4, 512, FEAT), BF),
             pltpu.VMEM((4, ROWS, 512), BF),
             pltpu.VMEM((512, HD), BF),
@@ -648,24 +695,7 @@
             *ring_scratch(ROWS),
             dma(2, 3), dma(2, 3), dma(2, 3), dma(2, 3),
             dma(16), dma(16), dma(16), dma(16), dma(16), dma(16),
-            dma(2), dma(2), dma(8), dma(8), dma(2, 4, 2), dma(2, 4, 2), dma(6),
-        ],
-        compiler_params=pltpu.CompilerParams(
-            collective_id=0, has_side_effects=True, vmem_limit_bytes=40 << 20
-        ),
-        name="mixer",
-    )(
-        head_rates, doc_lengths, query_rows, key_rows, value_rows, attn_gain.reshape(1, -1),
-        out_weight, residual, moe_gain.reshape(1, -1), ids,
-    )
-    return pl.pallas_call(
-        experts,
-        out_shape=jax.ShapeDtypeStruct((ROWS, FEAT), BF),
-        in_specs=[VM] * 5 + [ANY] * 3,
-        out_specs=VM,
-        scratch_shapes=[
-            pltpu.VMEM((FEAT + HID, D), BF),
-            pltpu.VMEM((HID, D), BF),
+            dma(1), dma(1), dma(4), dma(4), dma(8), dma(8), dma(2, 4, 2), dma(2, 4, 2), dma(12),
             pltpu.VMEM((BLOCKS, CAP, FEAT), BF),
             pltpu.VMEM((16, BLOCKS, CAP, FEAT), BF),
             pltpu.VMEM((SLOTS, 4 * FEAT), BF),
@@ -680,12 +710,13 @@
             dma(16), dma(16), dma(1), dma(1), dma(8), dma(8), dma(2, 4, 2), dma(2, 4, 2), dma(6),
         ],
         compiler_params=pltpu.CompilerParams(
-            collective_id=1, has_side_effects=True, vmem_limit_bytes=60 << 20
+            collective_id=0, has_side_effects=True, vmem_limit_bytes=67043328
         ),
-        name="experts",
+        name="layer",
     )(
-        h, ids_p, gains, ids, expert_weights.T,
-        gate_weight[0].T, up_weight[0].T, down_weight[0],
+        head_rates, doc_lengths, query_rows, key_rows, value_rows, attn_gain.reshape(1, -1),
+        out_weight, residual, moe_gain, expert_ids.T,
+        gate_weight[0].T, up_weight[0].T, down_weight[0], expert_weights.T,
     )
 
 

time: 139 us -> 122 us (0.88)
  local copies, waits for them, and re-layouts: 11.3 us -> 1.54 us
  Pallas kernels: 126 us -> 121 us
    unnamed x25 -> x1, local copies, waits for them, and re-layouts: 10.6 us -> 1.54 us
    pallas_call x2 -> x1, Pallas kernels: 126 us -> 121 us  [shards(): pl.pallas_call(layer, out_shape=jax.ShapeDtypeStruct((ROWS, FEAT), BF), i...]
where the time goes in v2:
time: 122 us
  Pallas kernels  121 us (99%)
  local copies, waits for them, and re-layouts  1.54 us (1%)
    pallas_call x1, Pallas kernels, shards(): pl.pallas_call(layer, out_shape=jax.ShapeDtypeStruct((ROWS, FEAT), BF), i...  121 us

profile of v2, /device:TPU:1, one launch (start us, length us, event | category | flops | bytes accessed | tf_op | source)
XLA Modules:
  0.0 122.1 jit_solution(5700206450510862638)
XLA Ops:
  0.0 120.5 %layer.1 = bf16[128,384]{1,0:T(8,128)(2,1)} custom-call(f32[64]{0:T(128)} %refs_0_.1, s32[4]{0:T(128)} %refs_1_.1, bf16[128,512]{1,0:T(8,128)(2,1)} %refs_2_.1, bf16[128,512]{1,0:T(8,128)(2,1)} %refs_3_.1, bf16[128,512]{1,0:T(8,128)(2,1)} %refs_4_.1, f32[1,512]{1,0:T(1,128)} %bitcast.13, bf16[512,384]{1,0:T(8,128)(2,1)} %refs_6_.1, ...), custom_call_target="tpu_custom_call" | custom-call | tf_op jit(solution)/shard_map/layer/pallas_call | solution.py:668
  120.5 1.5 %copy.16 = bf16[128,384]{1,0:T(8,128)(2,1)} copy(bf16[128,384]{1,0:T(8,128)(2,1)} %layer.1) | data formatting | bytes 196608

commit v3 on v2

--- a/solution.py
+++ b/solution.py
@@ -12,6 +12,8 @@
 BLOCKS = 16
 ROWS = 128
 FEAT = 384
+NEAR = 256
+FAR = 128
 HID = 288
 SLOTS = BLOCKS * CAP
 CTX = ("ctx_0", "ctx_1")
@@ -159,7 +161,7 @@
         cp.start()
         self.sent.append(cp)
 
-    def run(self, produce):
+    def begin(self, produce):
         produce(0)
         self.swap(0)
         produce(1)
@@ -173,6 +175,8 @@
         self.send(0, 1, 1, self.local(1, 1))
         self.swapped(2)
         self.send(1, 1, 0, self.local(2, 0))
+
+    def rest(self, produce):
         for i in range(3, 8):
             produce(i)
             self.swap(i)
@@ -234,7 +238,6 @@
     heads = RingGather(hbuf, hss, hrs, x, lambda i: (y, i, z, k), 64)
     own_w = pltpu.make_async_copy(w, wbuf.at[y], loc.at[0])
     own_w.start()
-    sent += weights.first(0, w)
 
     handed = remote(res, resbuf, ps.at[0], pr.at[0], partner)
     kept = pltpu.make_async_copy(res, resbuf, loc.at[1])
@@ -308,7 +311,7 @@
         )
         cp.start()
         sent.append(cp)
-    sent += weights.first(1, w)
+    sent += weights.first(0, w)
 
     loads[4].wait()
     loads[5].wait()
@@ -342,11 +345,9 @@
         )
         cp.start()
         sent.append(cp)
-    for d in range(2):
-        for part in range(2):
-            weights.arrived(d, part)
-    for d in range(2):
-        sent.append(weights.forward(d))
+    sent += weights.first(1, w)
+    weights.arrived(0, 0)
+    sent.append(weights.forward(0))
     own_onward.wait()
     for i in range(1, 16):
         ref = incoming.at[(me - i + 16) % 16]
@@ -364,6 +365,8 @@
     hbuf[x] = within[...].astype(BF)
     sent += heads.first(0, hbuf.at[x])
     sent += heads.first(1, hbuf.at[x])
+    weights.arrived(1, 1)
+    sent.append(weights.forward(1))
     heads.arrived(0, 0)
     sent.append(heads.forward(0))
     heads.arrived(1, 1)
@@ -371,6 +374,8 @@
     heads.arrived(0, 1)
     heads.arrived(1, 0)
     own_w.wait()
+    weights.arrived(0, 1)
+    weights.arrived(1, 0)
     for d in range(2):
         weights.forwarded(d)
     for d in range(2):
@@ -385,7 +390,8 @@
         out[i] = jnp.dot(hbuf[pair + 1 - k], wide, preferred_element_type=F32).astype(BF)
         own[i] = jnp.dot(hbuf[pair + k], wide, preferred_element_type=F32).astype(BF)
 
-    total.run(produce)
+    total.begin(produce)
+    total.rest(produce)
 
     @pl.when(low != x)
     def _():
@@ -427,30 +433,46 @@
 
 
 def experts(
-    wts, wgu, wd, weight_loads, h, ids_all, gains,
+    wts, wga, wgb, wda, wdb, weights_here, h, ids_all, gains,
     o_ref,
-    ds, xb, lhs, acc, squares, act, hn, qs, rb,
+    pick, ds, xb, hz, dsb, xb2, lhs, acc, squares, act, hn, qs, rb,
+    ownb, outb, gotb, qsb, rb2, pb, gb,
     own, out, got, tbuf, rbuf,
     dss, dsr, fs, fr, cs, cr, qss, qsr, ps, pr, xs, xr, ts, tr, loc,
+    b1s, b1r, b2s, b2r, os, osr, ws, wr, b3s, b3r, b4s, b4r,
 ):
     spot = y, x, z, k = place()
     me, t = 4 * y + x, 2 * z + k
     low, partner = partner_of(*spot)
     peer = (y, x, z, 1 - k)
     sent = []
-    hit0, hit1 = slot_hits(ids_all[low])
-    pick = jnp.where(hit0 | hit1, 1.0, 0.0).astype(BF)
-    picked = jnp.dot(pick, h[...], preferred_element_type=F32)
-    ds[...] = picked.reshape(BLOCKS, CAP, FEAT).astype(BF)
+
+    def push(cp):
+        cp.start()
+        sent.append(cp)
+
+    def at_ctx(c):
+        return (c // 4, c % 4, z, k)
+
+    def column_major(c):
+        return 4 * (c % 4) + c // 4
+
+    hz[z] = h[:, NEAR:]
+    for i in range(1, 8):
+        push(remote(hz.at[z], hz.at[z], b1s.at[i], b1r.at[i], (y, x, (z + i) % 8, k)))
+
+    for j in range(2):
+        hit0, hit1 = slot_hits(ids_all[2 * j + k])
+        pick[j] = jnp.where(hit0 | hit1, 1.0, 0.0).astype(BF)
+    picked = jnp.dot(pick[z % 2], h[:, :NEAR], preferred_element_type=F32)
+    ds[...] = picked.reshape(BLOCKS, CAP, NEAR).astype(BF)
 
     mine = 4 * x + y
     own_rows = pltpu.make_async_copy(ds.at[me], xb.at[t, mine], loc.at[3])
     own_rows.start()
     for i in range(1, 16):
         to = (me + i) % 16
-        cp = remote(ds.at[to], xb.at[t, mine], dss.at[i], dsr.at[i], (to // 4, to % 4, z, k))
-        cp.start()
-        sent.append(cp)
+        push(remote(ds.at[to], xb.at[t, mine], dss.at[i], dsr.at[i], at_ctx(to)))
     handed = remote(h, hn, ps.at[0], pr.at[0], partner)
     kept = pltpu.make_async_copy(h, hn, loc.at[4])
 
@@ -464,8 +486,7 @@
 
     own_rows.wait()
     for i in range(1, 16):
-        c = (me - i + 16) % 16
-        ref = xb.at[t, 4 * (c % 4) + c // 4]
+        ref = xb.at[t, column_major((me - i + 16) % 16)]
         remote(ref, ref, dss.at[i], dsr.at[i], peer).wait_recv()
 
     def half(zz, kk, part):
@@ -477,10 +498,6 @@
 
     def over(slot, part, ref):
         return remote(ref, ref, cs.at[slot, part], cr.at[slot, part], peer)
-
-    def push(cp):
-        cp.start()
-        sent.append(cp)
 
     def crossed(slot, dist):
         for part in range(2):
@@ -492,23 +509,55 @@
         push(ring(1, 0, part, ref))
         push(over(0, part, ref))
 
-    wgu[HID:FEAT, :] = jnp.zeros((FEAT - HID, D), BF)
+    for i in range(1, 8):
+        ref = hz.at[(z - i + 8) % 8]
+        remote(ref, ref, b1s.at[i], b1r.at[i], peer).wait_recv()
+    for j in range(2):
+        wide = jnp.concatenate([hz[2 * i + j] for i in range(4)], axis=1)
+        chosen = jnp.dot(pick[j], wide, preferred_element_type=F32)
+        dsb[:, j] = chosen.reshape(BLOCKS, CAP, 4 * FAR).astype(BF)
+    own_far = pltpu.make_async_copy(dsb.at[me], xb2.at[k, mine], loc.at[0])
+    own_far.start()
+    for i in range(1, 16):
+        to = (me + i) % 16
+        push(remote(dsb.at[to], xb2.at[k, mine], b2s.at[i], b2r.at[i], at_ctx(to)))
+
+    for w in (wga, wgb):
+        w[HID:FEAT, :] = jnp.zeros((FEAT - HID, w.shape[1]), BF)
     acc[...] = jnp.zeros_like(acc)
     squares[...] = jnp.zeros_like(squares)
 
+    def load_rows(piece, xp, gain, first):
+        rows = slice(96 * xp, 96 * xp + 96)
+        width = gain.shape[1]
+        piece = piece.astype(F32).reshape(96, width)
+        sq = piece * piece
+        add = sq[:, 0:128]
+        for i in range(1, width // 128):
+            add += sq[:, 128 * i : 128 * i + 128]
+        squares[rows, :] += add
+        lhs[rows, first : first + width] = (piece * gain).astype(BF)
+
+    def product(depth, w):
+        acc[...] += lax.dot_general(
+            lhs[:, :depth], w, (((1,), (1,)), ((), ())), preferred_element_type=F32
+        )
+
     def multiply(group):
         for xx in range(4):
-            gain = gains[4 * group + xx]
+            gain = gains[4 * group + xx][:, :NEAR]
             for xp in range(4):
-                rows = slice(96 * xp, 96 * xp + 96)
-                piece = xb[4 * group + xp, 4 * xx : 4 * xx + 4].astype(F32).reshape(96, FEAT)
-                sq = piece * piece
-                squares[rows, :] += sq[:, 0:128] + sq[:, 128:256] + sq[:, 256:384]
-                lhs[rows, xx * FEAT : (xx + 1) * FEAT] = (piece * gain).astype(BF)
-        cols = pl.ds(pl.multiple_of(group * 1536, 1536), 1536)
-        acc[...] += lax.dot_general(
-            lhs[...], wgu[:, cols], (((1,), (1,)), ((), ())), preferred_element_type=F32
-        )
+                load_rows(xb[4 * group + xp, 4 * xx : 4 * xx + 4], xp, gain, xx * NEAR)
+        cols = pl.ds(pl.multiple_of(group * 4 * NEAR, 4 * NEAR), 4 * NEAR)
+        product(4 * NEAR, wga[:, cols])
+
+    def multiply_far():
+        for xx in range(4):
+            gain = jnp.concatenate([gains[4 * i + xx][:, NEAR:] for i in range(4)], axis=1)
+            for xp in range(4):
+                piece = xb2[xp % 2, 4 * xx : 4 * xx + 4, xp // 2]
+                load_rows(piece, xp, gain, xx * 4 * FAR)
+        product(16 * FAR, wgb[...])
 
     side = jnp.where(z % 2 == 0, 3, 1)
     pair = z // 2
@@ -525,14 +574,20 @@
             crossed(0, 0)
             crossed(1, -1)
             crossed(2, 1)
-            weight_loads[0].wait()
-            weight_loads[1].wait()
+            weights_here(0)
             multiply(pair)
         elif s == 2:
             crossed(3, -2)
             crossed(4, 2)
             multiply((pair + side) % 4)
         else:
+            own_far.wait()
+            ref = xb2.at[k, mine]
+            push(remote(ref, ref, os.at[0], osr.at[0], peer))
+            for i in range(1, 16):
+                ref = xb2.at[k, column_major((me - i + 16) % 16)]
+                remote(ref, ref, b2s.at[i], b2r.at[i], peer).wait_recv()
+                push(remote(ref, ref, os.at[i], osr.at[i], peer))
             crossed(5, -3)
             crossed(6, 3)
             multiply((pair + 4 - side) % 4)
@@ -540,6 +595,10 @@
         ref = half(z + 4, k, d)
         ring(d, 3, d, ref).wait_recv()
         push(over(7, d, ref))
+    for i in range(16):
+        ref = xb2.at[1 - k, column_major((me - i + 16) % 16)]
+        remote(ref, ref, os.at[i], osr.at[i], peer).wait_recv()
+    multiply_far()
     crossed(7, 4)
     multiply((pair + 2) % 4)
 
@@ -548,7 +607,16 @@
     gate = acc[:, :HID] * scale
     lifted = acc[:, FEAT:] * scale
     act[...] = (gate / (1.0 + jnp.exp(-gate)) * lifted).astype(BF)
-    weight_loads[2].wait()
+    weights_here(1)
+
+    def far_tile(lane):
+        cols = pl.ds(pl.multiple_of(lane * 8 * FAR, 8 * FAR), 8 * FAR)
+        return jnp.dot(act[...], wdb[:, cols], preferred_element_type=F32).astype(BF)
+
+    outb[...] = far_tile(1 - k)
+    swap = remote(outb, gotb, ws.at[0], wr.at[0], peer)
+    push(swap)
+    ownb[...] = far_tile(k)
 
     total = RingSum(spot, SLOTS, own, out, got, tbuf, rbuf, xs, xr, ts, tr)
 
@@ -556,34 +624,54 @@
         chunk = (z + ORDER[i]) % 8
 
         def tile(lane):
-            cols = pl.ds(pl.multiple_of((2 * chunk + lane) * FEAT, FEAT), FEAT)
-            return jnp.dot(act[...], wd[:, cols], preferred_element_type=F32).astype(BF)
+            cols = pl.ds(pl.multiple_of((2 * chunk + lane) * NEAR, NEAR), NEAR)
+            return jnp.dot(act[...], wda[:, cols], preferred_element_type=F32).astype(BF)
 
         out[i] = tile(1 - k)
         own[i] = tile(k)
 
-    total.run(produce)
-    for part in range(2):
-        qs[part * 8 : part * 8 + 8] = total.result(part).reshape(8, CAP, FEAT).astype(BF)
-    own_back = pltpu.make_async_copy(qs.at[mine], rb.at[me], loc.at[5])
-    own_back.start()
+    total.begin(produce)
+    swap.wait_recv()
+    summed = ownb[...].astype(F32) + gotb[...].astype(F32)
+    qsb[...] = summed.reshape(BLOCKS, CAP, 8 * FAR).astype(BF)
+    own_home = pltpu.make_async_copy(qsb.at[mine], rb2.at[me], loc.at[1])
+    own_home.start()
     for i in range(1, 16):
         to = (me + i) % 16
-        push(
-            remote(
-                qs.at[4 * (to % 4) + to // 4],
-                rb.at[me],
-                qss.at[i],
-                qsr.at[i],
-                (to // 4, to % 4, z, k),
-            )
-        )
-    weight_loads[3].wait()
+        push(remote(qsb.at[column_major(to)], rb2.at[me], b3s.at[i], b3r.at[i], at_ctx(to)))
+    total.rest(produce)
+
+    weights_here(2)
     hit0, hit1 = slot_hits(ids_all[x])
     part_of = jnp.where(hit0, wts[0:1, :], 0.0) + jnp.where(hit1, wts[1:2, :], 0.0)
     coarse = part_of.astype(BF)
     fine = (part_of - coarse.astype(F32)).astype(BF)
 
+    def combine(ref):
+        back = ref[...].astype(F32).reshape(SLOTS, ref.shape[2]).astype(BF)
+        dims = (((0,), (0,)), ((), ()))
+        mixture = lax.dot_general(coarse, back, dims, preferred_element_type=F32)
+        return mixture + lax.dot_general(fine, back, dims, preferred_element_type=F32)
+
+    own_home.wait()
+    for i in range(1, 16):
+        ref = rb2.at[(me - i + 16) % 16]
+        remote(ref, ref, b3s.at[i], b3r.at[i], peer).wait_recv()
+    far_mix = combine(rb2)
+    for i in range(8):
+        pb[i] = far_mix[:, FAR * i : FAR * i + FAR].astype(BF)
+    for i in range(1, 8):
+        to = (z + i) % 8
+        push(remote(pb.at[to], gb.at[i], b4s.at[i], b4r.at[i], (y, x, to, k)))
+
+    for part in range(2):
+        qs[part * 8 : part * 8 + 8] = total.result(part).reshape(8, CAP, NEAR).astype(BF)
+    own_back = pltpu.make_async_copy(qs.at[mine], rb.at[me], loc.at[5])
+    own_back.start()
+    for i in range(1, 16):
+        to = (me + i) % 16
+        push(remote(qs.at[column_major(to)], rb.at[me], qss.at[i], qsr.at[i], at_ctx(to)))
+
     @pl.when(low != x)
     def _():
         handed.wait()
@@ -592,15 +680,16 @@
     def _():
         kept.wait()
 
+    far_sum = hn[:, NEAR:].astype(F32) + pb[z].astype(F32)
+    for i in range(1, 8):
+        remote(gb.at[i], gb.at[i], b4s.at[i], b4r.at[i], peer).wait_recv()
+        far_sum += gb[i].astype(F32)
+    o_ref[:, NEAR:] = far_sum.astype(BF)
     own_back.wait()
     for i in range(1, 16):
         ref = rb.at[(me - i + 16) % 16]
         remote(ref, ref, qss.at[i], qsr.at[i], peer).wait_recv()
-    back = rb[...].astype(F32).reshape(SLOTS, FEAT).astype(BF)
-    dims = (((0,), (0,)), ((), ()))
-    mixture = lax.dot_general(coarse, back, dims, preferred_element_type=F32)
-    mixture += lax.dot_general(fine, back, dims, preferred_element_type=F32)
-    o_ref[...] = (hn[...].astype(F32) + mixture).astype(BF)
+    o_ref[:, :NEAR] = (hn[:, :NEAR].astype(F32) + combine(rb)).astype(BF)
     return sent + total.sent
 
 
@@ -613,31 +702,47 @@
         return taken
 
     wg_hbm, wu_hbm, wd_hbm, wts_hbm = ins[10:]
-    wgu, wd, wts, weight_sems = take(4)
+    wga, wgb, wda, wdb, wts, wsem = take(6)
     early = take(6)
     passed = h, ids_all, gains = take(3)
     mix_scratch = take(8)
     mix_ring = take(5)
     mix_sems = take(19)
-    moe_scratch = take(9)
+    moe_scratch = take(20)
     moe_ring = take(5)
-    moe_sems = take(15)
-    weight_loads = [
-        pltpu.make_async_copy(wg_hbm, wgu.at[pl.ds(0, HID)], weight_sems.at[0]),
-        pltpu.make_async_copy(wu_hbm, wgu.at[pl.ds(FEAT, HID)], weight_sems.at[1]),
-        pltpu.make_async_copy(wd_hbm, wd, weight_sems.at[2]),
-        pltpu.make_async_copy(wts_hbm, wts, weight_sems.at[3]),
-    ]
+    moe_sems = take(27)
+    stages = ([], [], [])
+
+    def load(stage, src, dst):
+        n = sum(len(a) for a in stages)
+        stages[stage].append(pltpu.make_async_copy(src, dst, wsem.at[n]))
+
+    for c in range(16):
+        near, far = pl.ds(FEAT * c, NEAR), pl.ds(FEAT * c + NEAR, FAR)
+        spot = FAR * (4 * (c % 4) + c // 4)
+        for src, row in ((wg_hbm, 0), (wu_hbm, FEAT)):
+            rows = pl.ds(row, HID)
+            load(0, src.at[:, near], wga.at[rows, pl.ds(NEAR * c, NEAR)])
+            load(0, src.at[:, far], wgb.at[rows, pl.ds(spot, FAR)])
+        load(1, wd_hbm.at[:, near], wda.at[:, pl.ds(NEAR * c, NEAR)])
+        spot = FAR * (8 * (c % 2) + c // 2)
+        load(1, wd_hbm.at[:, far], wdb.at[:, pl.ds(spot, FAR)])
+    load(2, wts_hbm, wts)
 
     def start_weights():
-        for cp in weight_loads:
-            cp.start()
+        for stage in stages:
+            for cp in stage:
+                cp.start()
+
+    def weights_here(stage):
+        for cp in stages[stage]:
+            cp.wait()
 
     sent = mixer(
         *ins[:10], *early, *passed, *mix_scratch, *mix_ring, *mix_sems, start_weights
     )
     sent += experts(
-        wts, wgu, wd, weight_loads, *passed, o_ref, *moe_scratch, *moe_ring, *moe_sems
+        wts, wga, wgb, wda, wdb, weights_here, *passed, o_ref, *moe_scratch, *moe_ring, *moe_sems
     )
     for cp in sent:
         cp.wait_send()
@@ -647,14 +752,14 @@
     return pltpu.SemaphoreType.DMA(shape)
 
 
-def ring_scratch(rows):
+def ring_scratch(rows, width):
     half = rows // 2
     return [
-        pltpu.VMEM((8, rows, FEAT), BF),
-        pltpu.VMEM((8, rows, FEAT), BF),
-        pltpu.VMEM((8, rows, FEAT), BF),
-        pltpu.VMEM((2, 4, 2, half, FEAT), BF),
-        pltpu.VMEM((2, 4, 2, half, FEAT), BF),
+        pltpu.VMEM((8, rows, width), BF),
+        pltpu.VMEM((8, rows, width), BF),
+        pltpu.VMEM((8, rows, width), BF),
+        pltpu.VMEM((2, 4, 2, half, width), BF),
+        pltpu.VMEM((2, 4, 2, half, width), BF),
     ]
 
 
@@ -671,10 +776,12 @@
         in_specs=[ANY] * 14,
         out_specs=pl.BlockSpec(memory_space=pltpu.VMEM),
         scratch_shapes=[
-            pltpu.VMEM((FEAT + HID, D), BF),
-            pltpu.VMEM((HID, D), BF),
+            pltpu.VMEM((FEAT + HID, 16 * NEAR), BF),
+            pltpu.VMEM((FEAT + HID, 16 * FAR), BF),
+            pltpu.VMEM((HID, 16 * NEAR), BF),
+            pltpu.VMEM((HID, 16 * FAR), BF),
             pltpu.VMEM((2, ROWS), F32),
-            dma(4),
+            dma(97),
             pltpu.SMEM((64,), F32),
             pltpu.SMEM((4,), jnp.int32),
             pltpu.VMEM((ROWS, 512), BF),
@@ -692,22 +799,35 @@
             pltpu.VMEM((16, 32, HD), BF),
             pltpu.VMEM((ROWS, FEAT), BF),
             pltpu.VMEM((ROWS, 512), F32),
-            *ring_scratch(ROWS),
+            *ring_scratch(ROWS, FEAT),
             dma(2, 3), dma(2, 3), dma(2, 3), dma(2, 3),
             dma(16), dma(16), dma(16), dma(16), dma(16), dma(16),
             dma(1), dma(1), dma(4), dma(4), dma(8), dma(8), dma(2, 4, 2), dma(2, 4, 2), dma(12),
-            pltpu.VMEM((BLOCKS, CAP, FEAT), BF),
-            pltpu.VMEM((16, BLOCKS, CAP, FEAT), BF),
-            pltpu.VMEM((SLOTS, 4 * FEAT), BF),
+            pltpu.VMEM((2, SLOTS, ROWS), BF),
+            pltpu.VMEM((BLOCKS, CAP, NEAR), BF),
+            pltpu.VMEM((16, BLOCKS, CAP, NEAR), BF),
+            pltpu.VMEM((8, ROWS, FAR), BF),
+            pltpu.VMEM((BLOCKS, 2, CAP, 4 * FAR), BF),
+            pltpu.VMEM((2, BLOCKS, 2, CAP, 4 * FAR), BF),
+            pltpu.VMEM((SLOTS, 16 * FAR), BF),
             pltpu.VMEM((SLOTS, FEAT + HID), F32),
             pltpu.VMEM((SLOTS, 128), F32),
             pltpu.VMEM((SLOTS, HID), BF),
             pltpu.VMEM((ROWS, FEAT), BF),
-            pltpu.VMEM((BLOCKS, CAP, FEAT), BF),
-            pltpu.VMEM((BLOCKS, CAP, FEAT), BF),
-            *ring_scratch(SLOTS),
+            pltpu.VMEM((BLOCKS, CAP, NEAR), BF),
+            pltpu.VMEM((BLOCKS, CAP, NEAR), BF),
+            pltpu.VMEM((SLOTS, 8 * FAR), BF),
+            pltpu.VMEM((SLOTS, 8 * FAR), BF),
+            pltpu.VMEM((SLOTS, 8 * FAR), BF),
+            pltpu.VMEM((BLOCKS, CAP, 8 * FAR), BF),
+            pltpu.VMEM((BLOCKS, CAP, 8 * FAR), BF),
+            pltpu.VMEM((8, ROWS, FAR), BF),
+            pltpu.VMEM((8, ROWS, FAR), BF),
+            *ring_scratch(SLOTS, NEAR),
             dma(16), dma(16), dma(2, 4, 2), dma(2, 4, 2), dma(8, 2), dma(8, 2),
             dma(16), dma(16), dma(1), dma(1), dma(8), dma(8), dma(2, 4, 2), dma(2, 4, 2), dma(6),
+            dma(8), dma(8), dma(16), dma(16), dma(16), dma(16), dma(1), dma(1),
+            dma(16), dma(16), dma(8), dma(8),
         ],
         compiler_params=pltpu.CompilerParams(
             collective_id=0, has_side_effects=True, vmem_limit_bytes=67043328

time: 122 us -> 111 us (0.910)
  Pallas kernels: 121 us -> 109 us
    pallas_call x1, Pallas kernels: 121 us -> 109 us  [shards(): pl.pallas_call(layer, out_shape=jax.ShapeDtypeStruct((ROWS, FEAT), BF), i...]
where the time goes in v3:
time: 111 us; the launch traced here: 110 us
  Pallas kernels  109 us (98%)
  local copies, waits for them, and re-layouts  1.54 us (1%)
    pallas_call x1, Pallas kernels, shards(): pl.pallas_call(layer, out_shape=jax.ShapeDtypeStruct((ROWS, FEAT), BF), i...  109 us

profile of v3, /device:TPU:1, one launch (start us, length us, event | category | flops | bytes accessed | tf_op | source)
XLA Modules:
  0.0 110.1 jit_solution(2871938867677115177)
XLA Ops:
  0.0 108.6 %layer.1 = bf16[128,384]{1,0:T(8,128)(2,1)} custom-call(f32[64]{0:T(128)} %refs_0_.1, s32[4]{0:T(128)} %refs_1_.1, bf16[128,512]{1,0:T(8,128)(2,1)} %refs_2_.1, bf16[128,512]{1,0:T(8,128)(2,1)} %refs_3_.1, bf16[128,512]{1,0:T(8,128)(2,1)} %refs_4_.1, f32[1,512]{1,0:T(1,128)} %bitcast.13, bf16[512,384]{1,0:T(8,128)(2,1)} %refs_6_.1, ...), custom_call_target="tpu_custom_call" | custom-call | tf_op jit(solution)/shard_map/layer/pallas_call | solution.py:773
  108.6 1.5 %copy.16 = bf16[128,384]{1,0:T(8,128)(2,1)} copy(bf16[128,384]{1,0:T(8,128)(2,1)} %layer.1) | data formatting | bytes 196608

commit v4 on v3

v4 whole, which is shorter than its diff:
```python
import jax
import jax.numpy as jnp
from jax import lax
from jax.experimental import pallas as pl
from jax.experimental.pallas import tpu as pltpu
from jax.sharding import Mesh
from jax.sharding import PartitionSpec as P

D = 6144
HD = 128
CAP = 24
BLOCKS = 16
ROWS = 128
FEAT = 384
NEAR = 256
FAR = 128
HID = 288
SLOTS = BLOCKS * CAP
CTX = ("ctx_0", "ctx_1")
TP = ("tp_0", "tp_1")
AXES = CTX + TP
ORDER = (4, 3, 5, 2, 6, 1, 7, 0)
HOPS = [(d, s, p) for d in range(2) for s in range(4) for p in range(2) if s > 0 or p == d]
STEPS = [(d, s, p) for d in range(2) for s in range(4) for p in range(2) if s < 3 or p == d]
BF = jnp.bfloat16
F32 = jnp.float32


def remote(src, dst, send_sem, recv_sem, to):
    return pltpu.make_async_remote_copy(
        src_ref=src,
        dst_ref=dst,
        send_sem=send_sem,
        recv_sem=recv_sem,
        device_id=to,
        device_id_type=pl.DeviceIdType.MESH,
    )


def place():
    return tuple(lax.axis_index(a) for a in AXES)


def partner_of(y, x, z, k):
    low = 2 * (z % 2) + k
    return low, (y, low, 2 * (z // 2) + x // 2, x % 2)


def greet(y, x, z, k):
    sem = pltpu.get_barrier_semaphore()
    for i in range(1, 16):
        c = (4 * y + x + i) % 16
        pl.semaphore_signal(
            sem, inc=1, device_id=(c // 4, c % 4, z, k), device_id_type=pl.DeviceIdType.MESH
        )
    for i in range(1, 16):
        t = (2 * z + k + i) % 16
        pl.semaphore_signal(
            sem, inc=1, device_id=(y, x, t // 2, t % 2), device_id_type=pl.DeviceIdType.MESH
        )
    low, partner = partner_of(y, x, z, k)

    @pl.when(low != x)
    def _():
        pl.semaphore_signal(sem, inc=1, device_id=partner, device_id_type=pl.DeviceIdType.MESH)

    pl.semaphore_wait(sem, 30 + ((low - x + 4) % 4 + 3) // 4)


class Sends:
    def __init__(self):
        self.open = []

    def drain_later(self, ref, sem):
        self.open.append((ref, sem))

    def drain(self, to):
        for ref, sem in self.open:
            remote(ref, ref, sem, sem, to).wait_send()


class RingGather:
    def __init__(self, buf, ssem, rsem, me, device_at, half, sends):
        self.buf, self.ssem, self.rsem = buf, ssem, rsem
        self.me, self.at, self.half = me, device_at, half
        sends.drain_later(buf.at[pl.ds(0, 3)], ssem.at[0])

    def piece(self, member, part):
        return self.buf.at[member % 4, pl.ds(part * self.half, self.half)]

    def first(self, d, part, own):
        remote(
            own.at[pl.ds(part * self.half, self.half)],
            self.piece(self.me, part),
            self.ssem.at[0],
            self.rsem.at[d, part],
            self.at((self.me + (1, -1)[d]) % 4),
        ).start()

    def along(self, d, slot, ref):
        return remote(
            ref, ref, self.ssem.at[0], self.rsem.at[d, slot], self.at((self.me + (1, -1)[d]) % 4)
        )

    def arrived(self, d, part):
        self.along(d, part, self.piece(self.me + 4 - (1, -1)[d], part)).wait_recv()

    def forward(self, d):
        self.along(d, 2, self.piece(self.me + 4 - (1, -1)[d], d)).start()

    def forwarded(self, d):
        self.along(d, 2, self.piece(self.me + 2, d)).wait_recv()


class RingSum:
    def __init__(self, spot, rows, own, out, got, tbuf, rbuf, xs, xr, ssem, rsem, sends):
        self.y, self.x, self.z, self.k = spot
        self.half = rows // 2
        self.own, self.out, self.got = own, out, got
        self.tbuf, self.rbuf = tbuf, rbuf
        self.xs, self.xr, self.ssem, self.rsem = xs, xr, ssem, rsem
        sends.drain_later(out, xs.at[0])
        sends.drain_later(tbuf, ssem.at[0])

    def swap(self, i):
        self.swapping(i).start()

    def swapping(self, i):
        return remote(
            self.out.at[i],
            self.got.at[i],
            self.xs.at[0],
            self.xr.at[i],
            (self.y, self.x, self.z, 1 - self.k),
        )

    def swapped(self, i):
        self.swapping(i).wait_recv()

    def local(self, i, part):
        rows = pl.ds(part * self.half, self.half)
        return self.own[i, rows, :].astype(F32) + self.got[i, rows, :].astype(F32)

    def hop(self, d, s, part):
        to = (self.z + (1, 7)[d]) % 8
        return remote(
            self.tbuf.at[HOPS.index((d, s, part))],
            self.rbuf.at[HOPS.index((d, s, part))],
            self.ssem.at[0],
            self.rsem.at[HOPS.index((d, s, part))],
            (self.y, self.x, to, self.k),
        )

    def send(self, d, s, part, value):
        self.tbuf[HOPS.index((d, s, part))] = value.astype(BF)
        self.hop(d, s, part).start()

    def came(self, d, s, part):
        return self.rbuf[HOPS.index((d, s, part))].astype(F32)

    def begin(self, produce):
        produce(0)
        self.swap(0)
        produce(1)
        self.swap(1)
        produce(2)
        self.swap(2)
        self.swapped(0)
        self.send(0, 0, 0, self.local(0, 0))
        self.send(1, 0, 1, self.local(0, 1))
        self.swapped(1)
        self.send(0, 1, 1, self.local(1, 1))
        self.swapped(2)
        self.send(1, 1, 0, self.local(2, 0))

    def rest(self, produce):
        for i in range(3, 8):
            produce(i)
            self.swap(i)
        self.hop(0, 0, 0).wait_recv()
        self.send(0, 1, 0, self.local(1, 0) + self.came(0, 0, 0))
        self.hop(1, 0, 1).wait_recv()
        self.send(1, 1, 1, self.local(2, 1) + self.came(1, 0, 1))
        for s in (2, 3):
            self.swapped(2 * s - 1)
            self.swapped(2 * s)
            for j in range(2):
                for d in range(2):
                    part = (1 - j) if d == 0 else j
                    self.hop(d, s - 1, part).wait_recv()
                    self.send(
                        d,
                        s,
                        part,
                        self.local(2 * s - 1 + d, part) + self.came(d, s - 1, part),
                    )
        self.swapped(7)

    def result(self, part):
        self.hop(0, 3, part).wait_recv()
        self.hop(1, 3, part).wait_recv()
        return (
            self.local(7, part)
            + self.came(0, 3, part)
            + self.came(1, 3, part)
        )


def mixer(
    rates_hbm, docs_hbm, q_hbm, k_hbm, v_hbm, again_hbm, w, res, mgain, ids,
    rates, docs, q, k_in, v, again,
    h_out, ids_all, gain_out,
    wbuf, hbuf, state, arrived, onward, incoming, resbuf, within,
    own, out, got, tbuf, rbuf,
    wss, wrs, hss, hrs, a1s, a1r, a2s, a2r, gs, gr, ps, pr, ids_s, ids_r, xs, xr, ts, tr, loc, start_weights, sends,
):
    spot = y, x, z, k = place()
    me, t = 4 * y + x, 2 * z + k
    low, partner = partner_of(*spot)
    loads = [
        pltpu.make_async_copy(a, b, loc.at[6 + i])
        for i, (a, b) in enumerate(
            (
                (k_hbm, k_in), (v_hbm, v), (rates_hbm, rates), (docs_hbm, docs), (q_hbm, q),
                (again_hbm, again),
            )
        )
    ]
    for cp in loads:
        cp.start()
    greet(*spot)

    weights = RingGather(wbuf, wss, wrs, y, lambda i: (i, x, z, k), 256, sends)
    heads = RingGather(hbuf, hss, hrs, x, lambda i: (y, i, z, k), 64, sends)
    own_w = pltpu.make_async_copy(w, wbuf.at[y], loc.at[0])
    own_w.start()

    handed = remote(res, resbuf, ps.at[0], pr.at[0], partner)
    kept = pltpu.make_async_copy(res, resbuf, loc.at[1])

    @pl.when(low != x)
    def _():
        handed.start()

    @pl.when(low == x)
    def _():
        kept.start()

    own_ids = pltpu.make_async_copy(ids, ids_all.at[x], loc.at[2])
    own_ids.start()
    for i in range(1, 4):
        remote(ids, ids_all.at[x], ids_s.at[0], ids_r.at[0], (y, (x + i) % 4, z, k)).start()
    sends.drain_later(ids_all.at[pl.ds(0, 3)], ids_s.at[0])

    own_gain = pltpu.make_async_copy(mgain, gain_out.at[t, 0], loc.at[3])
    own_gain.start()
    for i in range(1, 16):
        to = (t + i) % 16
        remote(mgain, gain_out.at[t, 0], gs.at[0], gr.at[0], (y, x, to // 2, to % 2)).start()
    sends.drain_later(gain_out.at[pl.ds(0, 15)], gs.at[0])

    start_weights()
    for cp in loads[:4]:
        cp.wait()
    start1 = docs[0]
    start2 = start1 + docs[1]
    start3 = start2 + docs[2]

    def seg(p):
        def past(s):
            return jnp.where(p >= s, 1, 0)

        base = jnp.where(p >= 0, 0, -1)
        return base + past(start1) + past(start2) + past(start3)

    first = me * ROWS
    last_seg = seg(first + ROWS - 1)
    before = seg(first - 1)
    row = lax.broadcasted_iota(jnp.int32, (ROWS, HD), 0)
    col = lax.broadcasted_iota(jnp.int32, (ROWS, HD), 1)
    seg_row, seg_col = seg(first + row), seg(first + col)
    rowf = row.astype(F32)
    at_end = jnp.where(seg_row == last_seg, 1.0, 0.0)
    for h in range(4):
        rate = rates[4 * t + h]
        cols = slice(h * HD, (h + 1) * HD)
        fading = at_end * jnp.exp(-rate * (ROWS - 1.0 - rowf))
        faded = (k_in[:, cols].astype(F32) * fading).astype(BF)
        state[h * HD : (h + 1) * HD, :] = lax.dot_general(
            faded, v[:, cols], (((0,), (0,)), ((), ())), preferred_element_type=F32
        ).astype(BF)

    own_state = pltpu.make_async_copy(
        state.at[pl.ds(pl.multiple_of(me * 32, 32), 32)], arrived.at[me], loc.at[4]
    )
    own_state.start()
    for i in range(1, 16):
        to = (me + i) % 16
        remote(
            state.at[pl.ds(pl.multiple_of(to * 32, 32), 32)],
            arrived.at[me],
            a1s.at[0],
            a1r.at[0],
            (to // 4, to % 4, z, k),
        ).start()
    sends.drain_later(arrived.at[pl.ds(0, 15)], a1s.at[0])
    weights.first(0, 0, w)
    weights.first(1, 1, w)

    loads[4].wait()
    loads[5].wait()
    allowed = jnp.where((row >= col) & (seg_row == seg_col), 1.0, 0.0)
    gap = jnp.maximum(row - col, 0).astype(F32)
    for h in range(4):
        rate = rates[4 * t + h]
        cols = slice(h * HD, (h + 1) * HD)
        scores = lax.dot_general(
            q[:, cols], k_in[:, cols], (((1,), (1,)), ((), ())), preferred_element_type=F32
        )
        mixed = (scores * (allowed * jnp.exp(-rate * gap))).astype(BF)
        within[:, cols] = jnp.dot(mixed, v[:, cols], preferred_element_type=F32)

    own_state.wait()
    peer = (y, x, z, 1 - k)

    def receive(ref, sem):
        remote(ref, ref, sem, sem, peer).wait_recv()

    receive(arrived.at[pl.ds(0, 15)], a1r.at[0])
    decay = jnp.exp(jnp.zeros((32, HD), F32) - rates[4 * t + y] * ROWS)
    running = jnp.zeros((32, HD), F32)
    for b in range(BLOCKS):
        onward[b] = running.astype(BF)
        same = seg(jnp.int32(b * ROWS + ROWS - 1)) == seg(jnp.int32(b * ROWS - 1))
        running = running * (decay * jnp.where(same, 1.0, 0.0)) + arrived[b].astype(F32)
    own_onward = pltpu.make_async_copy(onward.at[me], incoming.at[me], loc.at[5])
    own_onward.start()
    for i in range(1, 16):
        to = (me + i) % 16
        remote(
            onward.at[to], incoming.at[me], a2s.at[0], a2r.at[0], (to // 4, to % 4, z, k)
        ).start()
    sends.drain_later(onward.at[pl.ds(0, 15)], a2s.at[0])
    for d in range(2):
        weights.arrived(d, d)
        weights.forward(d)
    for d in range(2):
        weights.first(d, 1 - d, w)
    own_onward.wait()
    receive(incoming.at[pl.ds(0, 15)], a2r.at[0])

    reached = jnp.where(seg_row == before, 1.0, 0.0)
    for h in range(4):
        rate = rates[4 * t + h]
        cols = slice(h * HD, (h + 1) * HD)
        inc = incoming[4 * h : 4 * h + 4].reshape(HD, HD)
        inter = jnp.dot(q[:, cols], inc, preferred_element_type=F32)
        both = within[:, cols] + inter * (reached * jnp.exp(-rate * (rowf + 1.0)))
        scale = lax.rsqrt(jnp.mean(both * both, axis=1, keepdims=True) + 1e-06)
        within[:, cols] = both * scale * again[:, cols]
    hbuf[x] = within[...].astype(BF)
    for part in range(2):
        for d in range(2):
            heads.first(d, part if d == 0 else 1 - part, hbuf.at[x])
    for d in range(2):
        heads.arrived(d, d)
        heads.forward(d)
    for d in range(2):
        heads.arrived(d, 1 - d)
    own_w.wait()
    for d in range(2):
        weights.arrived(d, 1 - d)
        weights.forwarded(d)
    for d in range(2):
        heads.forwarded(d)

    total = RingSum(spot, ROWS, own, out, got, tbuf, rbuf, xs, xr, ts, tr, sends)

    def produce(i):
        chunk = (z + ORDER[i]) % 8
        pair = 2 * (chunk % 2)
        wide = wbuf[chunk // 2]
        out[i] = jnp.dot(hbuf[pair + 1 - k], wide, preferred_element_type=F32).astype(BF)
        own[i] = jnp.dot(hbuf[pair + k], wide, preferred_element_type=F32).astype(BF)

    total.begin(produce)
    total.rest(produce)

    @pl.when(low != x)
    def _():
        handed.wait()

    @pl.when(low == x)
    def _():
        kept.wait()

    for part in range(2):
        rows = slice(part * 64, part * 64 + 64)
        h_out[rows, :] = (resbuf[rows, :].astype(F32) + total.result(part)).astype(BF)
    own_gain.wait()
    receive(gain_out.at[pl.ds(0, 15)], gr.at[0])
    own_ids.wait()
    receive(ids_all.at[pl.ds(0, 3)], ids_r.at[0])


def slot_hits(ids):
    expert = lax.broadcasted_iota(jnp.int32, (BLOCKS, CAP, ROWS), 0).reshape(SLOTS, ROWS)
    place_in = lax.broadcasted_iota(jnp.int32, (BLOCKS, CAP, ROWS), 1).reshape(SLOTS, ROWS)
    hit0 = expert == ids[0:1, :]
    hit1 = expert == ids[1:2, :]
    named = jnp.where(hit0 | hit1, 1.0, 0.0)
    earlier = lax.broadcasted_iota(jnp.int32, (ROWS, ROWS), 0)
    later = lax.broadcasted_iota(jnp.int32, (ROWS, ROWS), 1)
    rank = jnp.dot(
        named.astype(BF),
        jnp.where(earlier < later, 1.0, 0.0).astype(BF),
        preferred_element_type=F32,
    )
    here = rank == place_in.astype(F32)
    return hit0 & here, hit1 & here


def experts(
    wts, wgu, wd, loads, h, ids_all, gains,
    o_ref,
    pick, ds, xb, hz, dsb, xb2, lhs, acc, squares, act, hn, qs, rb,
    ownb, outb, gotb, qsb, rb2, pb, gb,
    own, out, got, tbuf, rbuf,
    dss, dsr, fs, fr, cs, cr, qss, qsr, ps, pr, xs, xr, ts, tr, loc,
    b1s, b1r, b2s, b2r, os, osr, ws, wr, b3s, b3r, b4s, b4r,
    sends,
):
    spot = y, x, z, k = place()
    me, t = 4 * y + x, 2 * z + k
    low, partner = partner_of(*spot)
    peer = (y, x, z, 1 - k)

    def receive(ref, sem):
        remote(ref, ref, sem, sem, peer).wait_recv()

    def at_ctx(c):
        return (c // 4, c % 4, z, k)

    def column_major(c):
        return 4 * (c % 4) + c // 4

    hz[z] = h[:, NEAR:]
    for i in range(1, 8):
        remote(hz.at[z], hz.at[z], b1s.at[0], b1r.at[0], (y, x, (z + i) % 8, k)).start()
    sends.drain_later(hz.at[pl.ds(0, 7)], b1s.at[0])

    for j in range(2):
        hit0, hit1 = slot_hits(ids_all[2 * j + k])
        pick[j] = jnp.where(hit0 | hit1, 1.0, 0.0).astype(BF)
    picked = jnp.dot(pick[z % 2], h[:, :NEAR], preferred_element_type=F32)
    ds[...] = picked.reshape(BLOCKS, CAP, NEAR).astype(BF)

    mine = 4 * x + y
    own_rows = pltpu.make_async_copy(ds.at[me], xb.at[t, mine], loc.at[3])
    own_rows.start()
    for i in range(1, 16):
        to = (me + i) % 16
        remote(ds.at[to], xb.at[t, mine], dss.at[0], dsr.at[0], at_ctx(to)).start()
    sends.drain_later(ds.at[pl.ds(0, 15)], dss.at[0])
    handed = remote(h, hn, ps.at[0], pr.at[0], partner)
    kept = pltpu.make_async_copy(h, hn, loc.at[4])

    @pl.when(low != x)
    def _():
        handed.start()

    @pl.when(low == x)
    def _():
        kept.start()

    own_rows.wait()
    receive(xb.at[t, pl.ds(0, 15)], dsr.at[0])

    def half(zz, kk, part):
        return xb.at[2 * ((zz + 8) % 8) + kk, pl.ds(part * 8, 8)]

    def ring(d, s, part, ref):
        to = (z + (1, 7)[d]) % 8
        return remote(
            ref, ref, fs.at[0], fr.at[STEPS.index((d, s, part))], (y, x, to, k)
        )

    def over(slot, ref):
        remote(ref, ref, cs.at[0], cr.at[slot], peer).start()

    def crossed(slot, dist):
        receive(xb.at[2 * ((z + dist + 8) % 8) + 1 - k], cr.at[slot])

    sends.drain_later(xb.at[pl.ds(0, 7)], fs.at[0])
    sends.drain_later(xb.at[pl.ds(0, 8)], cs.at[0])
    for part in range(2):
        ref = half(z, k, part)
        ring(0, 0, part, ref).start()
        ring(1, 0, part, ref).start()
        over(0, ref)

    receive(hz.at[pl.ds(0, 7)], b1r.at[0])
    for j in range(2):
        wide = jnp.concatenate([hz[2 * i + j] for i in range(4)], axis=1)
        chosen = jnp.dot(pick[j], wide, preferred_element_type=F32)
        dsb[:, j] = chosen.reshape(BLOCKS, CAP, 4 * FAR).astype(BF)
    own_far = pltpu.make_async_copy(dsb.at[me], xb2.at[k, mine], loc.at[0])
    own_far.start()
    for i in range(1, 16):
        to = (me + i) % 16
        remote(dsb.at[to], xb2.at[k, mine], b2s.at[0], b2r.at[0], at_ctx(to)).start()
    sends.drain_later(dsb.at[pl.ds(0, 15)], b2s.at[0])

    wgu[HID:FEAT, :] = jnp.zeros((FEAT - HID, D), BF)
    acc[...] = jnp.zeros_like(acc)
    squares[...] = jnp.zeros_like(squares)

    def columns(ref, tile, first, width):
        return ref[:, pl.ds(pl.multiple_of(tile * FEAT + first, 128), width)]

    def load_rows(piece, xp, gain, first):
        rows = slice(96 * xp, 96 * xp + 96)
        width = gain.shape[1]
        piece = piece.astype(F32).reshape(96, width)
        sq = piece * piece
        add = sq[:, 0:128]
        for i in range(1, width // 128):
            add += sq[:, 128 * i : 128 * i + 128]
        squares[rows, :] += add
        lhs[rows, first : first + width] = (piece * gain).astype(BF)

    def product(depth, w):
        acc[...] += lax.dot_general(
            lhs[:, :depth], w, (((1,), (1,)), ((), ())), preferred_element_type=F32
        )

    def multiply(group):
        for xx in range(4):
            gain = gains[4 * group + xx][:, :NEAR]
            for xp in range(4):
                load_rows(xb[4 * group + xp, 4 * xx : 4 * xx + 4], xp, gain, xx * NEAR)
        product(
            4 * NEAR,
            jnp.concatenate([columns(wgu, 4 * group + xx, 0, NEAR) for xx in range(4)], axis=1),
        )

    def multiply_far():
        for xx in range(4):
            gain = jnp.concatenate([gains[4 * i + xx][:, NEAR:] for i in range(4)], axis=1)
            for xp in range(4):
                piece = xb2[xp % 2, 4 * xx : 4 * xx + 4, xp // 2]
                load_rows(piece, xp, gain, xx * 4 * FAR)
        product(
            16 * FAR,
            jnp.concatenate(
                [columns(wgu, 4 * i + xx, NEAR, FAR) for xx in range(4) for i in range(4)], axis=1
            ),
        )

    side = jnp.where(z % 2 == 0, 3, 1)
    pair = z // 2
    def step(s):
        for part in range(2):
            for d in range(2):
                ref = half(z + (-s if d == 0 else s), k, part)
                ring(d, s - 1, part, ref).wait_recv()
                if s < 3 or part == d:
                    ring(d, s, part, ref).start()
                over(2 * s - 1 + d, ref)

    step(1)
    step(2)
    loads[0].wait()
    loads[1].wait()
    crossed(0, 0)
    crossed(1, -1)
    crossed(2, 1)
    multiply(pair)
    step(3)
    crossed(3, -2)
    crossed(4, 2)
    multiply((pair + side) % 4)
    own_far.wait()
    receive(xb2.at[k, pl.ds(0, 15)], b2r.at[0])
    hand_over = remote(xb2.at[k], xb2.at[k], os.at[0], osr.at[0], peer)
    hand_over.start()
    sends.drain_later(xb2.at[k], os.at[0])
    crossed(5, -3)
    crossed(6, 3)
    multiply((pair + 4 - side) % 4)
    for d in range(2):
        ref = half(z + 4, k, d)
        ring(d, 3, d, ref).wait_recv()
        over(7, ref)
    receive(xb2.at[1 - k], osr.at[0])
    multiply_far()
    crossed(7, 4)
    multiply((pair + 2) % 4)

    total_sq = jnp.sum(squares[...], axis=1, keepdims=True)
    scale = lax.rsqrt(total_sq / D + 1e-05)
    gate = acc[:, :HID] * scale
    lifted = acc[:, FEAT:] * scale
    act[...] = (gate / (1.0 + jnp.exp(-gate)) * lifted).astype(BF)
    loads[2].wait()

    def far_tile(lane):
        cols = jnp.concatenate([columns(wd, 2 * i + lane, NEAR, FAR) for i in range(8)], axis=1)
        return jnp.dot(act[...], cols, preferred_element_type=F32).astype(BF)

    outb[...] = far_tile(1 - k)
    swap = remote(outb, gotb, ws.at[0], wr.at[0], peer)
    swap.start()
    sends.drain_later(outb, ws.at[0])
    ownb[...] = far_tile(k)

    total = RingSum(spot, SLOTS, own, out, got, tbuf, rbuf, xs, xr, ts, tr, sends)

    def produce(i):
        chunk = (z + ORDER[i]) % 8

        def tile(lane):
            cols = columns(wd, 2 * chunk + lane, 0, NEAR)
            return jnp.dot(act[...], cols, preferred_element_type=F32).astype(BF)

        out[i] = tile(1 - k)
        own[i] = tile(k)

    total.begin(produce)
    swap.wait_recv()
    summed = ownb[...].astype(F32) + gotb[...].astype(F32)
    qsb[...] = summed.reshape(BLOCKS, CAP, 8 * FAR).astype(BF)
    own_home = pltpu.make_async_copy(qsb.at[mine], rb2.at[me], loc.at[1])
    own_home.start()
    for i in range(1, 16):
        to = (me + i) % 16
        remote(qsb.at[column_major(to)], rb2.at[me], b3s.at[0], b3r.at[0], at_ctx(to)).start()
    sends.drain_later(qsb.at[pl.ds(0, 15)], b3s.at[0])
    total.rest(produce)

    loads[3].wait()
    hit0, hit1 = slot_hits(ids_all[x])
    part_of = jnp.where(hit0, wts[0:1, :], 0.0) + jnp.where(hit1, wts[1:2, :], 0.0)
    coarse = part_of.astype(BF)
    fine = (part_of - coarse.astype(F32)).astype(BF)

    def combine(ref):
        back = ref[...].astype(F32).reshape(SLOTS, ref.shape[2]).astype(BF)
        dims = (((0,), (0,)), ((), ()))
        mixture = lax.dot_general(coarse, back, dims, preferred_element_type=F32)
        return mixture + lax.dot_general(fine, back, dims, preferred_element_type=F32)

    own_home.wait()
    receive(rb2.at[pl.ds(0, 15)], b3r.at[0])
    far_mix = combine(rb2)
    for i in range(8):
        pb[i] = far_mix[:, FAR * i : FAR * i + FAR].astype(BF)
    for i in range(1, 8):
        to = (z + i) % 8
        remote(pb.at[to], gb.at[i], b4s.at[0], b4r.at[0], (y, x, to, k)).start()
    sends.drain_later(pb.at[pl.ds(0, 7)], b4s.at[0])

    for part in range(2):
        qs[part * 8 : part * 8 + 8] = total.result(part).reshape(8, CAP, NEAR).astype(BF)
    own_back = pltpu.make_async_copy(qs.at[mine], rb.at[me], loc.at[5])
    own_back.start()
    for i in range(1, 16):
        to = (me + i) % 16
        remote(qs.at[column_major(to)], rb.at[me], qss.at[0], qsr.at[0], at_ctx(to)).start()
    sends.drain_later(qs.at[pl.ds(0, 15)], qss.at[0])

    @pl.when(low != x)
    def _():
        handed.wait()

    @pl.when(low == x)
    def _():
        kept.wait()

    far_sum = hn[:, NEAR:].astype(F32) + pb[z].astype(F32)
    receive(gb.at[pl.ds(1, 7)], b4r.at[0])
    for i in range(1, 8):
        far_sum += gb[i].astype(F32)
    o_ref[:, NEAR:] = far_sum.astype(BF)
    own_back.wait()
    receive(rb.at[pl.ds(0, 15)], qsr.at[0])
    o_ref[:, :NEAR] = (hn[:, :NEAR].astype(F32) + combine(rb)).astype(BF)


def layer(*refs):
    ins, o_ref, refs = refs[:14], refs[14], list(refs[15:])

    def take(n):
        taken = refs[:n]
        del refs[:n]
        return taken

    wg_hbm, wu_hbm, wd_hbm, wts_hbm = ins[10:]
    wgu, wd, wts, wsem = take(4)
    early = take(6)
    passed = h, ids_all, gains = take(3)
    mix_scratch = take(8)
    mix_ring = take(5)
    mix_sems = take(19)
    moe_scratch = take(20)
    moe_ring = take(5)
    moe_sems = take(27)
    loads = [
        pltpu.make_async_copy(wg_hbm, wgu.at[pl.ds(0, HID)], wsem.at[0]),
        pltpu.make_async_copy(wu_hbm, wgu.at[pl.ds(FEAT, HID)], wsem.at[1]),
        pltpu.make_async_copy(wd_hbm, wd, wsem.at[2]),
        pltpu.make_async_copy(wts_hbm, wts, wsem.at[3]),
    ]

    def start_weights():
        for cp in loads:
            cp.start()

    sends = Sends()
    mixer(
        *ins[:10], *early, *passed, *mix_scratch, *mix_ring, *mix_sems, start_weights, sends
    )
    experts(wts, wgu, wd, loads, *passed, o_ref, *moe_scratch, *moe_ring, *moe_sems, sends)
    y, x, z, k = place()
    sends.drain((y, x, z, 1 - k))


def dma(*shape):
    return pltpu.SemaphoreType.DMA(shape)


def ring_scratch(rows, width):
    half = rows // 2
    return [
        pltpu.VMEM((8, rows, width), BF),
        pltpu.VMEM((8, rows, width), BF),
        pltpu.VMEM((8, rows, width), BF),
        pltpu.VMEM((14, half, width), BF),
        pltpu.VMEM((14, half, width), BF),
    ]


ANY = pl.BlockSpec(memory_space=pl.ANY)


def shards(
    residual, query_rows, key_rows, value_rows, head_rates, doc_lengths, attn_gain, out_weight,
    moe_gain, expert_ids, expert_weights, gate_weight, up_weight, down_weight,
):
    return pl.pallas_call(
        layer,
        out_shape=jax.ShapeDtypeStruct((ROWS, FEAT), BF),
        in_specs=[ANY] * 14,
        out_specs=pl.BlockSpec(memory_space=pltpu.VMEM),
        scratch_shapes=[
            pltpu.VMEM((FEAT + HID, D), BF),
            pltpu.VMEM((HID, D), BF),
            pltpu.VMEM((2, ROWS), F32),
            dma(4),
            pltpu.SMEM((64,), F32),
            pltpu.SMEM((4,), jnp.int32),
            pltpu.VMEM((ROWS, 512), BF),
            pltpu.VMEM((ROWS, 512), BF),
            pltpu.VMEM((ROWS, 512), BF),
            pltpu.VMEM((1, 512), F32),
            pltpu.VMEM((ROWS, FEAT), BF),
            pltpu.VMEM((4, 2, ROWS), jnp.int32),
            pltpu.VMEM((16, 1, FEAT), F32),
            pltpu.VMEM((4, 512, FEAT), BF),
            pltpu.VMEM((4, ROWS, 512), BF),
            pltpu.VMEM((512, HD), BF),
            pltpu.VMEM((16, 32, HD), BF),
            pltpu.VMEM((16, 32, HD), BF),
            pltpu.VMEM((16, 32, HD), BF),
            pltpu.VMEM((ROWS, FEAT), BF),
            pltpu.VMEM((ROWS, 512), F32),
            *ring_scratch(ROWS, FEAT),
            dma(1), dma(2, 3), dma(1), dma(2, 3),
            dma(1), dma(1), dma(1), dma(1), dma(1), dma(1),
            dma(1), dma(1), dma(1), dma(1), dma(1), dma(8), dma(1), dma(14), dma(12),
            pltpu.VMEM((2, SLOTS, ROWS), BF),
            pltpu.VMEM((BLOCKS, CAP, NEAR), BF),
            pltpu.VMEM((16, BLOCKS, CAP, NEAR), BF),
            pltpu.VMEM((8, ROWS, FAR), BF),
            pltpu.VMEM((BLOCKS, 2, CAP, 4 * FAR), BF),
            pltpu.VMEM((2, BLOCKS, 2, CAP, 4 * FAR), BF),
            pltpu.VMEM((SLOTS, 16 * FAR), BF),
            pltpu.VMEM((SLOTS, FEAT + HID), F32),
            pltpu.VMEM((SLOTS, 128), F32),
            pltpu.VMEM((SLOTS, HID), BF),
            pltpu.VMEM((ROWS, FEAT), BF),
            pltpu.VMEM((BLOCKS, CAP, NEAR), BF),
            pltpu.VMEM((BLOCKS, CAP, NEAR), BF),
            pltpu.VMEM((SLOTS, 8 * FAR), BF),
            pltpu.VMEM((SLOTS, 8 * FAR), BF),
            pltpu.VMEM((SLOTS, 8 * FAR), BF),
            pltpu.VMEM((BLOCKS, CAP, 8 * FAR), BF),
            pltpu.VMEM((BLOCKS, CAP, 8 * FAR), BF),
            pltpu.VMEM((8, ROWS, FAR), BF),
            pltpu.VMEM((8, ROWS, FAR), BF),
            *ring_scratch(SLOTS, NEAR),
            dma(1), dma(1), dma(1), dma(14), dma(1), dma(8),
            dma(1), dma(1), dma(1), dma(1), dma(1), dma(8), dma(1), dma(14), dma(6),
            dma(1), dma(1), dma(1), dma(1), dma(1), dma(1), dma(1), dma(1),
            dma(1), dma(1), dma(1), dma(1),
        ],
        compiler_params=pltpu.CompilerParams(
            collective_id=0, has_side_effects=True, vmem_limit_bytes=67043328
        ),
        name="layer",
    )(
        head_rates, doc_lengths, query_rows, key_rows, value_rows, attn_gain.reshape(1, -1),
        out_weight, residual, moe_gain, expert_ids.T,
        gate_weight[0].T, up_weight[0].T, down_weight[0], expert_weights.T,
    )


def solution(mesh):
    finer = Mesh(mesh.devices.reshape(4, 4, 8, 2), AXES)
    placed = (
        P(CTX, TP), P(CTX, TP), P(CTX, TP), P(CTX, TP), P(), P(), P(TP), P(TP, CTX), P(TP),
        P(CTX, None), P(CTX, None), P(CTX, None, TP), P(CTX, None, TP), P(CTX, TP, None),
    )
    return jax.shard_map(shards, mesh=finer, in_specs=placed, out_specs=P(CTX, TP), check_vma=False)
```

time: 111 us -> 109 us (0.982)
  no operation moved by 1% of the time
where the time goes in v4:
time: 109 us
  Pallas kernels  108 us (99%)
  local copies, waits for them, and re-layouts  1.54 us (1%)
    pallas_call x1, Pallas kernels, shards(): pl.pallas_call(layer, out_shape=jax.ShapeDtypeStruct((ROWS, FEAT), BF), i...  108 us

profile of v4, /device:TPU:1, one launch (start us, length us, event | category | flops | bytes accessed | tf_op | source)
XLA Modules:
  0.0 109.3 jit_solution(12138431087421610158)
XLA Ops:
  0.0 107.7 %layer.1 = bf16[128,384]{1,0:T(8,128)(2,1)} custom-call(f32[64]{0:T(128)} %refs_0_.1, s32[4]{0:T(128)} %refs_1_.1, bf16[128,512]{1,0:T(8,128)(2,1)} %refs_2_.1, bf16[128,512]{1,0:T(8,128)(2,1)} %refs_3_.1, bf16[128,512]{1,0:T(8,128)(2,1)} %refs_4_.1, f32[1,512]{1,0:T(1,128)} %bitcast.13, bf16[512,384]{1,0:T(8,128)(2,1)} %refs_6_.1, ...), custom_call_target="tpu_custom_call" | custom-call | tf_op jit(solution)/shard_map/layer/pallas_call | solution.py:750
  107.7 1.5 %copy.16 = bf16[128,384]{1,0:T(8,128)(2,1)} copy(bf16[128,384]{1,0:T(8,128)(2,1)} %layer.1) | data formatting | bytes 196608

commit v5 on v4

--- a/solution.py
+++ b/solution.py
@@ -20,7 +20,7 @@
 TP = ("tp_0", "tp_1")
 AXES = CTX + TP
 ORDER = (4, 3, 5, 2, 6, 1, 7, 0)
-HOPS = [(d, s, p) for d in range(2) for s in range(4) for p in range(2) if s > 0 or p == d]
+HOPS = [(d, s, p) for d in range(2) for s in range(4) for p in range(4) if s > 0 or p // 2 == d]
 STEPS = [(d, s, p) for d in range(2) for s in range(4) for p in range(2) if s < 3 or p == d]
 BF = jnp.bfloat16
 F32 = jnp.float32
@@ -115,7 +115,7 @@
 class RingSum:
     def __init__(self, spot, rows, own, out, got, tbuf, rbuf, xs, xr, ssem, rsem, sends):
         self.y, self.x, self.z, self.k = spot
-        self.half = rows // 2
+        self.quarter = rows // 4
         self.own, self.out, self.got = own, out, got
         self.tbuf, self.rbuf = tbuf, rbuf
         self.xs, self.xr, self.ssem, self.rsem = xs, xr, ssem, rsem
@@ -138,7 +138,7 @@
         self.swapping(i).wait_recv()
 
     def local(self, i, part):
-        rows = pl.ds(part * self.half, self.half)
+        rows = pl.ds(part * self.quarter, self.quarter)
         return self.own[i, rows, :].astype(F32) + self.got[i, rows, :].astype(F32)
 
     def hop(self, d, s, part):
@@ -158,42 +158,46 @@
     def came(self, d, s, part):
         return self.rbuf[HOPS.index((d, s, part))].astype(F32)
 
-    def begin(self, produce):
-        produce(0)
-        self.swap(0)
-        produce(1)
+    def begin(self, tile, aside=None, later=None):
+        self.make(tile, 0)
+        self.out[1] = tile(1, False)
         self.swap(1)
-        produce(2)
-        self.swap(2)
+        if aside:
+            aside()
         self.swapped(0)
-        self.send(0, 0, 0, self.local(0, 0))
-        self.send(1, 0, 1, self.local(0, 1))
-        self.swapped(1)
-        self.send(0, 1, 1, self.local(1, 1))
-        self.swapped(2)
-        self.send(1, 1, 0, self.local(2, 0))
-
-    def rest(self, produce):
-        for i in range(3, 8):
-            produce(i)
-            self.swap(i)
-        self.hop(0, 0, 0).wait_recv()
-        self.send(0, 1, 0, self.local(1, 0) + self.came(0, 0, 0))
-        self.hop(1, 0, 1).wait_recv()
-        self.send(1, 1, 1, self.local(2, 1) + self.came(1, 0, 1))
-        for s in (2, 3):
-            self.swapped(2 * s - 1)
-            self.swapped(2 * s)
+        for j in range(2):
+            for d in range(2):
+                self.send(d, 0, 2 * d + j, self.local(0, 2 * d + j))
+        self.own[1] = tile(1, True)
+        self.make(tile, 2)
+        if later:
+            later()
+        for d in range(2):
+            self.swapped(1 + d)
             for j in range(2):
+                part = 2 * (1 - d) + j
+                self.send(d, 1, part, self.local(1 + d, part))
+
+    def make(self, tile, i):
+        self.out[i] = tile(i, False)
+        self.swap(i)
+        self.own[i] = tile(i, True)
+
+    def rest(self, tile):
+        for s in (1, 2, 3):
+            for i in range(2 * s + 1, min(2 * s + 3, 8)):
+                self.make(tile, i)
+            if s > 1:
+                self.swapped(2 * s - 1)
+                self.swapped(2 * s)
+            for j in range(4):
                 for d in range(2):
-                    part = (1 - j) if d == 0 else j
+                    part = (j + 2 * (1 - d)) % 4
+                    if s == 1 and part // 2 != d:
+                        continue
                     self.hop(d, s - 1, part).wait_recv()
-                    self.send(
-                        d,
-                        s,
-                        part,
-                        self.local(2 * s - 1 + d, part) + self.came(d, s - 1, part),
-                    )
+                    value = self.local(2 * s - 1 + d, part) + self.came(d, s - 1, part)
+                    self.send(d, s, part, value)
         self.swapped(7)
 
     def result(self, part):
@@ -376,15 +380,13 @@
 
     total = RingSum(spot, ROWS, own, out, got, tbuf, rbuf, xs, xr, ts, tr, sends)
 
-    def produce(i):
+    def tile(i, mine):
         chunk = (z + ORDER[i]) % 8
-        pair = 2 * (chunk % 2)
-        wide = wbuf[chunk // 2]
-        out[i] = jnp.dot(hbuf[pair + 1 - k], wide, preferred_element_type=F32).astype(BF)
-        own[i] = jnp.dot(hbuf[pair + k], wide, preferred_element_type=F32).astype(BF)
-
-    total.begin(produce)
-    total.rest(produce)
+        row = 2 * (chunk % 2) + (k if mine else 1 - k)
+        return jnp.dot(hbuf[row], wbuf[chunk // 2], preferred_element_type=F32).astype(BF)
+
+    total.begin(tile)
+    total.rest(tile)
 
     @pl.when(low != x)
     def _():
@@ -394,8 +396,8 @@
     def _():
         kept.wait()
 
-    for part in range(2):
-        rows = slice(part * 64, part * 64 + 64)
+    for part in range(4):
+        rows = slice(part * 32, part * 32 + 32)
         h_out[rows, :] = (resbuf[rows, :].astype(F32) + total.result(part)).astype(BF)
     own_gain.wait()
     receive(gain_out.at[pl.ds(0, 15)], gr.at[0])
@@ -445,8 +447,11 @@
         return 4 * (c % 4) + c // 4
 
     hz[z] = h[:, NEAR:]
-    for i in range(1, 8):
-        remote(hz.at[z], hz.at[z], b1s.at[0], b1r.at[0], (y, x, (z + i) % 8, k)).start()
+    def along_z(ref, dist, sem):
+        remote(ref, ref, b1s.at[0], b1r.at[sem], (y, x, (z + dist) % 8, k)).start()
+
+    for dist, sem in ((2, 0), (6, 1), (1, 2), (7, 2)):
+        along_z(hz.at[z], dist, sem)
     sends.drain_later(hz.at[pl.ds(0, 7)], b1s.at[0])
 
     for j in range(2):
@@ -464,15 +469,11 @@
     sends.drain_later(ds.at[pl.ds(0, 15)], dss.at[0])
     handed = remote(h, hn, ps.at[0], pr.at[0], partner)
     kept = pltpu.make_async_copy(h, hn, loc.at[4])
-
-    @pl.when(low != x)
-    def _():
-        handed.start()
-
-    @pl.when(low == x)
-    def _():
-        kept.start()
-
+    for sem, dist in ((0, 6), (1, 2)):
+        spot_z = (z + dist) % 8
+        receive(hz.at[spot_z], b1r.at[sem])
+        along_z(hz.at[spot_z], (1, 7)[sem], 2)
+        along_z(hz.at[spot_z, pl.ds(64 * sem, 64)], (2, 6)[sem], 2)
     own_rows.wait()
     receive(xb.at[t, pl.ds(0, 15)], dsr.at[0])
 
@@ -499,7 +500,7 @@
         ring(1, 0, part, ref).start()
         over(0, ref)
 
-    receive(hz.at[pl.ds(0, 7)], b1r.at[0])
+    receive(hz.at[pl.ds(0, 5)], b1r.at[2])
     for j in range(2):
         wide = jnp.concatenate([hz[2 * i + j] for i in range(4)], axis=1)
         chosen = jnp.dot(pick[j], wide, preferred_element_type=F32)
@@ -577,14 +578,22 @@
     crossed(2, 1)
     multiply(pair)
     step(3)
+
+    @pl.when(low != x)
+    def _():
+        handed.start()
+
+    @pl.when(low == x)
+    def _():
+        kept.start()
+
+    own_far.wait()
+    receive(xb2.at[k, pl.ds(0, 15)], b2r.at[0])
+    remote(xb2.at[k], xb2.at[k], os.at[0], osr.at[0], peer).start()
+    sends.drain_later(xb2.at[k], os.at[0])
     crossed(3, -2)
     crossed(4, 2)
     multiply((pair + side) % 4)
-    own_far.wait()
-    receive(xb2.at[k, pl.ds(0, 15)], b2r.at[0])
-    hand_over = remote(xb2.at[k], xb2.at[k], os.at[0], osr.at[0], peer)
-    hand_over.start()
-    sends.drain_later(xb2.at[k], os.at[0])
     crossed(5, -3)
     crossed(6, 3)
     multiply((pair + 4 - side) % 4)
@@ -608,25 +617,24 @@
         cols = jnp.concatenate([columns(wd, 2 * i + lane, NEAR, FAR) for i in range(8)], axis=1)
         return jnp.dot(act[...], cols, preferred_element_type=F32).astype(BF)
 
-    outb[...] = far_tile(1 - k)
     swap = remote(outb, gotb, ws.at[0], wr.at[0], peer)
-    swap.start()
     sends.drain_later(outb, ws.at[0])
-    ownb[...] = far_tile(k)
+
+    def aside():
+        outb[...] = far_tile(1 - k)
+        swap.start()
+
+    def later():
+        ownb[...] = far_tile(k)
 
     total = RingSum(spot, SLOTS, own, out, got, tbuf, rbuf, xs, xr, ts, tr, sends)
 
-    def produce(i):
+    def tile(i, mine):
         chunk = (z + ORDER[i]) % 8
-
-        def tile(lane):
-            cols = columns(wd, 2 * chunk + lane, 0, NEAR)
-            return jnp.dot(act[...], cols, preferred_element_type=F32).astype(BF)
-
-        out[i] = tile(1 - k)
-        own[i] = tile(k)
-
-    total.begin(produce)
+        cols = columns(wd, 2 * chunk + (k if mine else 1 - k), 0, NEAR)
+        return jnp.dot(act[...], cols, preferred_element_type=F32).astype(BF)
+
+    total.begin(tile, aside, later)
     swap.wait_recv()
     summed = ownb[...].astype(F32) + gotb[...].astype(F32)
     qsb[...] = summed.reshape(BLOCKS, CAP, 8 * FAR).astype(BF)
@@ -636,7 +644,7 @@
         to = (me + i) % 16
         remote(qsb.at[column_major(to)], rb2.at[me], b3s.at[0], b3r.at[0], at_ctx(to)).start()
     sends.drain_later(qsb.at[pl.ds(0, 15)], b3s.at[0])
-    total.rest(produce)
+    total.rest(tile)
 
     loads[3].wait()
     hit0, hit1 = slot_hits(ids_all[x])
@@ -660,13 +668,19 @@
         remote(pb.at[to], gb.at[i], b4s.at[0], b4r.at[0], (y, x, to, k)).start()
     sends.drain_later(pb.at[pl.ds(0, 7)], b4s.at[0])
 
-    for part in range(2):
-        qs[part * 8 : part * 8 + 8] = total.result(part).reshape(8, CAP, NEAR).astype(BF)
     own_back = pltpu.make_async_copy(qs.at[mine], rb.at[me], loc.at[5])
-    own_back.start()
-    for i in range(1, 16):
-        to = (me + i) % 16
-        remote(qs.at[column_major(to)], rb.at[me], qss.at[0], qsr.at[0], at_ctx(to)).start()
+    for part in range(4):
+        qs[part * 4 : part * 4 + 4] = total.result(part).reshape(4, CAP, NEAR).astype(BF)
+        for i in range(4):
+            row = (y + i) % 4
+            home = remote(
+                qs.at[4 * part + row], rb.at[me], qss.at[0], qsr.at[0], (row, part, z, k)
+            )
+            if i > 0:
+                home.start()
+            else:
+                pl.when(part != x)(home.start)
+                pl.when(part == x)(own_back.start)
     sends.drain_later(qs.at[pl.ds(0, 15)], qss.at[0])
 
     @pl.when(low != x)
@@ -730,13 +744,13 @@
 
 
 def ring_scratch(rows, width):
-    half = rows // 2
+    quarter = rows // 4
     return [
         pltpu.VMEM((8, rows, width), BF),
         pltpu.VMEM((8, rows, width), BF),
         pltpu.VMEM((8, rows, width), BF),
-        pltpu.VMEM((14, half, width), BF),
-        pltpu.VMEM((14, half, width), BF),
+        pltpu.VMEM((28, quarter, width), BF),
+        pltpu.VMEM((28, quarter, width), BF),
     ]
 
 
@@ -777,7 +791,7 @@
             *ring_scratch(ROWS, FEAT),
             dma(1), dma(2, 3), dma(1), dma(2, 3),
             dma(1), dma(1), dma(1), dma(1), dma(1), dma(1),
-            dma(1), dma(1), dma(1), dma(1), dma(1), dma(8), dma(1), dma(14), dma(12),
+            dma(1), dma(1), dma(1), dma(1), dma(1), dma(8), dma(1), dma(28), dma(12),
             pltpu.VMEM((2, SLOTS, ROWS), BF),
             pltpu.VMEM((BLOCKS, CAP, NEAR), BF),
             pltpu.VMEM((16, BLOCKS, CAP, NEAR), BF),
@@ -800,8 +814,8 @@
             pltpu.VMEM((8, ROWS, FAR), BF),
             *ring_scratch(SLOTS, NEAR),
             dma(1), dma(1), dma(1), dma(14), dma(1), dma(8),
-            dma(1), dma(1), dma(1), dma(1), dma(1), dma(8), dma(1), dma(14), dma(6),
-            dma(1), dma(1), dma(1), dma(1), dma(1), dma(1), dma(1), dma(1),
+            dma(1), dma(1), dma(1), dma(1), dma(1), dma(8), dma(1), dma(28), dma(6),
+            dma(1), dma(3), dma(1), dma(1), dma(1), dma(1), dma(1), dma(1),
             dma(1), dma(1), dma(1), dma(1),
         ],
         compiler_params=pltpu.CompilerParams(

time: 109 us -> 103 us (0.945)
  Pallas kernels: 108 us -> 101 us
    pallas_call x1, Pallas kernels: 108 us -> 101 us  [shards(): pl.pallas_call(layer, out_shape=jax.ShapeDtypeStruct((ROWS, FEAT), BF), i...]
where the time goes in v5:
time: 103 us
  Pallas kernels  101 us (98%)
  local copies, waits for them, and re-layouts  1.54 us (1%)
    pallas_call x1, Pallas kernels, shards(): pl.pallas_call(layer, out_shape=jax.ShapeDtypeStruct((ROWS, FEAT), BF), i...  101 us

profile of v5, /device:TPU:1, one launch (start us, length us, event | category | flops | bytes accessed | tf_op | source)
XLA Modules:
  0.0 103.0 jit_solution(12320480830378070287)
XLA Ops:
  0.0 101.4 %layer.1 = bf16[128,384]{1,0:T(8,128)(2,1)} custom-call(f32[64]{0:T(128)} %refs_0_.1, s32[4]{0:T(128)} %refs_1_.1, bf16[128,512]{1,0:T(8,128)(2,1)} %refs_2_.1, bf16[128,512]{1,0:T(8,128)(2,1)} %refs_3_.1, bf16[128,512]{1,0:T(8,128)(2,1)} %refs_4_.1, f32[1,512]{1,0:T(1,128)} %bitcast.13, bf16[512,384]{1,0:T(8,128)(2,1)} %refs_6_.1, ...), custom_call_target="tpu_custom_call" | custom-call | tf_op jit(solution)/shard_map/layer/pallas_call | solution.py:764
  101.4 1.5 %copy.16 = bf16[128,384]{1,0:T(8,128)(2,1)} copy(bf16[128,384]{1,0:T(8,128)(2,1)} %layer.1) | data formatting | bytes 196608

commit v6 on v5

--- a/solution.py
+++ b/solution.py
@@ -22,6 +22,10 @@
 ORDER = (4, 3, 5, 2, 6, 1, 7, 0)
 HOPS = [(d, s, p) for d in range(2) for s in range(4) for p in range(4) if s > 0 or p // 2 == d]
 STEPS = [(d, s, p) for d in range(2) for s in range(4) for p in range(2) if s < 3 or p == d]
+OFFSETS = sorted(
+    ((dy, dx) for dy in range(4) for dx in range(4) if dy or dx),
+    key=lambda o: -(min(o[0], 4 - o[0]) + min(o[1], 4 - o[1])),
+)
 BF = jnp.bfloat16
 F32 = jnp.float32
 
@@ -39,6 +43,10 @@
 
 def place():
     return tuple(lax.axis_index(a) for a in AXES)
+
+
+def others(y, x):
+    return [((y + dy) % 4, (x + dx) % 4) for dy, dx in OFFSETS]
 
 
 def partner_of(y, x, z, k):
@@ -298,8 +306,8 @@
         state.at[pl.ds(pl.multiple_of(me * 32, 32), 32)], arrived.at[me], loc.at[4]
     )
     own_state.start()
-    for i in range(1, 16):
-        to = (me + i) % 16
+    for ty, tx in others(y, x):
+        to = 4 * ty + tx
         remote(
             state.at[pl.ds(pl.multiple_of(to * 32, 32), 32)],
             arrived.at[me],
@@ -339,8 +347,8 @@
         running = running * (decay * jnp.where(same, 1.0, 0.0)) + arrived[b].astype(F32)
     own_onward = pltpu.make_async_copy(onward.at[me], incoming.at[me], loc.at[5])
     own_onward.start()
-    for i in range(1, 16):
-        to = (me + i) % 16
+    for ty, tx in others(y, x):
+        to = 4 * ty + tx
         remote(
             onward.at[to], incoming.at[me], a2s.at[0], a2r.at[0], (to // 4, to % 4, z, k)
         ).start()
@@ -426,7 +434,7 @@
     wts, wgu, wd, loads, h, ids_all, gains,
     o_ref,
     pick, ds, xb, hz, dsb, xb2, lhs, acc, squares, act, hn, qs, rb,
-    ownb, outb, gotb, qsb, rb2, pb, gb,
+    ownb, outb, gotb, qsb, rb2, pb, gb, tb,
     own, out, got, tbuf, rbuf,
     dss, dsr, fs, fr, cs, cr, qss, qsr, ps, pr, xs, xr, ts, tr, loc,
     b1s, b1r, b2s, b2r, os, osr, ws, wr, b3s, b3r, b4s, b4r,
@@ -463,8 +471,8 @@
     mine = 4 * x + y
     own_rows = pltpu.make_async_copy(ds.at[me], xb.at[t, mine], loc.at[3])
     own_rows.start()
-    for i in range(1, 16):
-        to = (me + i) % 16
+    for ty, tx in others(y, x):
+        to = 4 * ty + tx
         remote(ds.at[to], xb.at[t, mine], dss.at[0], dsr.at[0], at_ctx(to)).start()
     sends.drain_later(ds.at[pl.ds(0, 15)], dss.at[0])
     handed = remote(h, hn, ps.at[0], pr.at[0], partner)
@@ -507,8 +515,8 @@
         dsb[:, j] = chosen.reshape(BLOCKS, CAP, 4 * FAR).astype(BF)
     own_far = pltpu.make_async_copy(dsb.at[me], xb2.at[k, mine], loc.at[0])
     own_far.start()
-    for i in range(1, 16):
-        to = (me + i) % 16
+    for ty, tx in others(y, x):
+        to = 4 * ty + tx
         remote(dsb.at[to], xb2.at[k, mine], b2s.at[0], b2r.at[0], at_ctx(to)).start()
     sends.drain_later(dsb.at[pl.ds(0, 15)], b2s.at[0])
 
@@ -640,8 +648,8 @@
     qsb[...] = summed.reshape(BLOCKS, CAP, 8 * FAR).astype(BF)
     own_home = pltpu.make_async_copy(qsb.at[mine], rb2.at[me], loc.at[1])
     own_home.start()
-    for i in range(1, 16):
-        to = (me + i) % 16
+    for ty, tx in others(y, x):
+        to = 4 * ty + tx
         remote(qsb.at[column_major(to)], rb2.at[me], b3s.at[0], b3r.at[0], at_ctx(to)).start()
     sends.drain_later(qsb.at[pl.ds(0, 15)], b3s.at[0])
     total.rest(tile)
@@ -663,9 +671,14 @@
     far_mix = combine(rb2)
     for i in range(8):
         pb[i] = far_mix[:, FAR * i : FAR * i + FAR].astype(BF)
-    for i in range(1, 8):
-        to = (z + i) % 8
-        remote(pb.at[to], gb.at[i], b4s.at[0], b4r.at[0], (y, x, to, k)).start()
+    def along(src, dst, sem, dist):
+        remote(src, dst, b4s.at[0], b4r.at[sem], (y, x, (z + dist + 8) % 8, k)).start()
+
+    for d, sign in enumerate((1, -1)):
+        rows = pl.ds(64 * d, 64)
+        along(pb.at[(z + 4) % 8, rows], gb.at[5 + 2 * d, rows], 2 + 2 * d, 2 * sign)
+        along(pb.at[(z + 3 * sign + 8) % 8], gb.at[4 + 2 * d], 1 + 2 * d, sign)
+        along(pb.at[(z + sign + 8) % 8], gb.at[d], 0, sign)
     sends.drain_later(pb.at[pl.ds(0, 7)], b4s.at[0])
 
     own_back = pltpu.make_async_copy(qs.at[mine], rb.at[me], loc.at[5])
@@ -682,6 +695,13 @@
                 pl.when(part != x)(home.start)
                 pl.when(part == x)(own_back.start)
     sends.drain_later(qs.at[pl.ds(0, 15)], qss.at[0])
+    for d, sign in enumerate((1, -1)):
+        rows = pl.ds(64 * d, 64)
+        receive(gb.at[4 + 2 * d], b4r.at[1 + 2 * d])
+        tb[d] = (pb[(z + 2 * sign + 8) % 8].astype(F32) + gb[4 + 2 * d].astype(F32)).astype(BF)
+        receive(gb.at[5 + 2 * d, rows], b4r.at[2 + 2 * d])
+        tb[d, rows, :] = (tb[d, rows, :].astype(F32) + gb[5 + 2 * d, rows, :].astype(F32)).astype(BF)
+        along(tb.at[d], gb.at[2 + d], 0, 2 * sign)
 
     @pl.when(low != x)
     def _():
@@ -692,8 +712,8 @@
         kept.wait()
 
     far_sum = hn[:, NEAR:].astype(F32) + pb[z].astype(F32)
-    receive(gb.at[pl.ds(1, 7)], b4r.at[0])
-    for i in range(1, 8):
+    receive(gb.at[pl.ds(0, 4)], b4r.at[0])
+    for i in range(4):
         far_sum += gb[i].astype(F32)
     o_ref[:, NEAR:] = far_sum.astype(BF)
     own_back.wait()
@@ -716,7 +736,7 @@
     mix_scratch = take(8)
     mix_ring = take(5)
     mix_sems = take(19)
-    moe_scratch = take(20)
+    moe_scratch = take(21)
     moe_ring = take(5)
     moe_sems = take(27)
     loads = [
@@ -812,11 +832,12 @@
             pltpu.VMEM((BLOCKS, CAP, 8 * FAR), BF),
             pltpu.VMEM((8, ROWS, FAR), BF),
             pltpu.VMEM((8, ROWS, FAR), BF),
+            pltpu.VMEM((2, ROWS, FAR), BF),
             *ring_scratch(SLOTS, NEAR),
             dma(1), dma(1), dma(1), dma(14), dma(1), dma(8),
             dma(1), dma(1), dma(1), dma(1), dma(1), dma(8), dma(1), dma(28), dma(6),
             dma(1), dma(3), dma(1), dma(1), dma(1), dma(1), dma(1), dma(1),
-            dma(1), dma(1), dma(1), dma(1),
+            dma(1), dma(1), dma(1), dma(5),
         ],
         compiler_params=pltpu.CompilerParams(
             collective_id=0, has_side_effects=True, vmem_limit_bytes=67043328

time: 103 us -> 101 us (0.981)
  Pallas kernels: 101 us -> 99.3 us
    pallas_call x1, Pallas kernels: 101 us -> 99.3 us  [shards(): pl.pallas_call(layer, out_shape=jax.ShapeDtypeStruct((ROWS, FEAT), BF), i...]
where the time goes in v6:
time: 101 us
  Pallas kernels  99.3 us (98%)
  local copies, waits for them, and re-layouts  1.54 us (2%)
    pallas_call x1, Pallas kernels, shards(): pl.pallas_call(layer, out_shape=jax.ShapeDtypeStruct((ROWS, FEAT), BF), i...  99.3 us

profile of v6, /device:TPU:1, one launch (start us, length us, event | category | flops | bytes accessed | tf_op | source)
XLA Modules:
  0.0 100.8 jit_solution(15398840217132373050)
XLA Ops:
  0.0 99.3 %layer.1 = bf16[128,384]{1,0:T(8,128)(2,1)} custom-call(f32[64]{0:T(128)} %refs_0_.1, s32[4]{0:T(128)} %refs_1_.1, bf16[128,512]{1,0:T(8,128)(2,1)} %refs_2_.1, bf16[128,512]{1,0:T(8,128)(2,1)} %refs_3_.1, bf16[128,512]{1,0:T(8,128)(2,1)} %refs_4_.1, f32[1,512]{1,0:T(1,128)} %bitcast.13, bf16[512,384]{1,0:T(8,128)(2,1)} %refs_6_.1, ...), custom_call_target="tpu_custom_call" | custom-call | tf_op jit(solution)/shard_map/layer/pallas_call | solution.py:784
  99.3 1.5 %copy.16 = bf16[128,384]{1,0:T(8,128)(2,1)} copy(bf16[128,384]{1,0:T(8,128)(2,1)} %layer.1) | data formatting | bytes 196608

commit v7 on v6

--- a/solution.py
+++ b/solution.py
@@ -26,6 +26,7 @@
     ((dy, dx) for dy in range(4) for dx in range(4) if dy or dx),
     key=lambda o: -(min(o[0], 4 - o[0]) + min(o[1], 4 - o[1])),
 )
+STAND = (0, 2, 1, 3)
 BF = jnp.bfloat16
 F32 = jnp.float32
 
@@ -354,10 +355,10 @@
         ).start()
     sends.drain_later(onward.at[pl.ds(0, 15)], a2s.at[0])
     for d in range(2):
+        weights.first(d, 1 - d, w)
+    for d in range(2):
         weights.arrived(d, d)
         weights.forward(d)
-    for d in range(2):
-        weights.first(d, 1 - d, w)
     own_onward.wait()
     receive(incoming.at[pl.ds(0, 15)], a2r.at[0])
 
@@ -451,9 +452,6 @@
     def at_ctx(c):
         return (c // 4, c % 4, z, k)
 
-    def column_major(c):
-        return 4 * (c % 4) + c // 4
-
     hz[z] = h[:, NEAR:]
     def along_z(ref, dist, sem):
         remote(ref, ref, b1s.at[0], b1r.at[sem], (y, x, (z + dist) % 8, k)).start()
@@ -469,6 +467,7 @@
     ds[...] = picked.reshape(BLOCKS, CAP, NEAR).astype(BF)
 
     mine = 4 * x + y
+    home_row = 4 * (2 * (x % 2) + x // 2) + y
     own_rows = pltpu.make_async_copy(ds.at[me], xb.at[t, mine], loc.at[3])
     own_rows.start()
     for ty, tx in others(y, x):
@@ -527,8 +526,8 @@
     def columns(ref, tile, first, width):
         return ref[:, pl.ds(pl.multiple_of(tile * FEAT + first, 128), width)]
 
-    def load_rows(piece, xp, gain, first):
-        rows = slice(96 * xp, 96 * xp + 96)
+    def load_rows(piece, stand, gain, first, into):
+        rows = pl.ds(stand * 96, 96)
         width = gain.shape[1]
         piece = piece.astype(F32).reshape(96, width)
         sq = piece * piece
@@ -536,30 +535,33 @@
         for i in range(1, width // 128):
             add += sq[:, 128 * i : 128 * i + 128]
         squares[rows, :] += add
-        lhs[rows, first : first + width] = (piece * gain).astype(BF)
-
-    def product(depth, w):
-        acc[...] += lax.dot_general(
-            lhs[:, :depth], w, (((1,), (1,)), ((), ())), preferred_element_type=F32
+        lhs[96 * into : 96 * into + 96, first : first + width] = (piece * gain).astype(BF)
+
+    def product(rows, depth, w):
+        acc[rows, :] += lax.dot_general(
+            lhs[: rows.size, :depth], w, (((1,), (1,)), ((), ())), preferred_element_type=F32
         )
 
     def multiply(group):
         for xx in range(4):
             gain = gains[4 * group + xx][:, :NEAR]
             for xp in range(4):
-                load_rows(xb[4 * group + xp, 4 * xx : 4 * xx + 4], xp, gain, xx * NEAR)
+                piece = xb[4 * group + xp, 4 * xx : 4 * xx + 4]
+                load_rows(piece, STAND[xp], gain, xx * NEAR, STAND[xp])
         product(
+            pl.ds(0, SLOTS),
             4 * NEAR,
             jnp.concatenate([columns(wgu, 4 * group + xx, 0, NEAR) for xx in range(4)], axis=1),
         )
 
-    def multiply_far():
+    def multiply_far(lane):
         for xx in range(4):
             gain = jnp.concatenate([gains[4 * i + xx][:, NEAR:] for i in range(4)], axis=1)
-            for xp in range(4):
-                piece = xb2[xp % 2, 4 * xx : 4 * xx + 4, xp // 2]
-                load_rows(piece, xp, gain, xx * 4 * FAR)
+            for j in range(2):
+                piece = xb2[lane, 4 * xx : 4 * xx + 4, j]
+                load_rows(piece, 2 * lane + j, gain, xx * 4 * FAR, j)
         product(
+            pl.ds(pl.multiple_of(lane * 192, 192), 192),
             16 * FAR,
             jnp.concatenate(
                 [columns(wgu, 4 * i + xx, NEAR, FAR) for xx in range(4) for i in range(4)], axis=1
@@ -602,6 +604,7 @@
     crossed(3, -2)
     crossed(4, 2)
     multiply((pair + side) % 4)
+    multiply_far(k)
     crossed(5, -3)
     crossed(6, 3)
     multiply((pair + 4 - side) % 4)
@@ -610,7 +613,7 @@
         ring(d, 3, d, ref).wait_recv()
         over(7, ref)
     receive(xb2.at[1 - k], osr.at[0])
-    multiply_far()
+    multiply_far(1 - k)
     crossed(7, 4)
     multiply((pair + 2) % 4)
 
@@ -646,11 +649,11 @@
     swap.wait_recv()
     summed = ownb[...].astype(F32) + gotb[...].astype(F32)
     qsb[...] = summed.reshape(BLOCKS, CAP, 8 * FAR).astype(BF)
-    own_home = pltpu.make_async_copy(qsb.at[mine], rb2.at[me], loc.at[1])
+    own_home = pltpu.make_async_copy(qsb.at[home_row], rb2.at[me], loc.at[1])
     own_home.start()
     for ty, tx in others(y, x):
         to = 4 * ty + tx
-        remote(qsb.at[column_major(to)], rb2.at[me], b3s.at[0], b3r.at[0], at_ctx(to)).start()
+        remote(qsb.at[4 * (2 * (tx % 2) + tx // 2) + ty], rb2.at[me], b3s.at[0], b3r.at[0], at_ctx(to)).start()
     sends.drain_later(qsb.at[pl.ds(0, 15)], b3s.at[0])
     total.rest(tile)
 
@@ -681,19 +684,19 @@
         along(pb.at[(z + sign + 8) % 8], gb.at[d], 0, sign)
     sends.drain_later(pb.at[pl.ds(0, 7)], b4s.at[0])
 
-    own_back = pltpu.make_async_copy(qs.at[mine], rb.at[me], loc.at[5])
+    own_back = pltpu.make_async_copy(qs.at[home_row], rb.at[me], loc.at[5])
     for part in range(4):
         qs[part * 4 : part * 4 + 4] = total.result(part).reshape(4, CAP, NEAR).astype(BF)
         for i in range(4):
             row = (y + i) % 4
             home = remote(
-                qs.at[4 * part + row], rb.at[me], qss.at[0], qsr.at[0], (row, part, z, k)
+                qs.at[4 * part + row], rb.at[me], qss.at[0], qsr.at[0], (row, STAND[part], z, k)
             )
             if i > 0:
                 home.start()
             else:
-                pl.when(part != x)(home.start)
-                pl.when(part == x)(own_back.start)
+                pl.when(STAND[part] != x)(home.start)
+                pl.when(STAND[part] == x)(own_back.start)
     sends.drain_later(qs.at[pl.ds(0, 15)], qss.at[0])
     for d, sign in enumerate((1, -1)):
         rows = pl.ds(64 * d, 64)

time: 101 us -> 101 us (level)
  no operation moved by 1% of the time
where the time goes in v7:
time: 101 us
  Pallas kernels  99.2 us (98%)
  local copies, waits for them, and re-layouts  1.54 us (2%)
    pallas_call x1, Pallas kernels, shards(): pl.pallas_call(layer, out_shape=jax.ShapeDtypeStruct((ROWS, FEAT), BF), i...  99.2 us

profile of v7, /device:TPU:1, one launch (start us, length us, event | category | flops | bytes accessed | tf_op | source)
XLA Modules:
  0.0 100.7 jit_solution(14344354912692662426)
XLA Ops:
  0.0 99.2 %layer.1 = bf16[128,384]{1,0:T(8,128)(2,1)} custom-call(f32[64]{0:T(128)} %refs_0_.1, s32[4]{0:T(128)} %refs_1_.1, bf16[128,512]{1,0:T(8,128)(2,1)} %refs_2_.1, bf16[128,512]{1,0:T(8,128)(2,1)} %refs_3_.1, bf16[128,512]{1,0:T(8,128)(2,1)} %refs_4_.1, f32[1,512]{1,0:T(1,128)} %bitcast.13, bf16[512,384]{1,0:T(8,128)(2,1)} %refs_6_.1, ...), custom_call_target="tpu_custom_call" | custom-call | tf_op jit(solution)/shard_map/layer/pallas_call | solution.py:787
  99.2 1.5 %copy.16 = bf16[128,384]{1,0:T(8,128)(2,1)} copy(bf16[128,384]{1,0:T(8,128)(2,1)} %layer.1) | data formatting | bytes 196608
